TPU v7x, 256 devices: a whole 4x4x8 slice. The times are simulated.
256 devices in a mesh: section: 4 (over x), expert: 64 (over y, z, core).
Axes of the slice: x: 4, y: 4, z: 8, core: 2. Of those that a mesh axis runs over, the one named last changes fastest.
Arguments:
- tokens: bfloat16 [2, 4096, 2560], P(None, 'expert'), may hold values from -6 to 6
- norm_gain: float32 [4, 2560], P('section'), may hold values from 0.1 to 1.9
- w_gate: bfloat16 [4, 2560, 24576], P('section', None, 'expert'), may hold values from -0.125 to 0.125
- w_up: bfloat16 [4, 2560, 24576], P('section', None, 'expert'), may hold values from -0.125 to 0.125
- w_down: bfloat16 [4, 24576, 2560], P('section', 'expert'), may hold values from -0.21875 to 0.21875
- route_ids: int32 [4, 2, 4096, 2], P('section', None, 'expert'), may hold values from 0 to 31, all different within a row; in each aligned block of 64 rows (0 to 63, 64 to 127, ..., all dimensions but the last counted through in order) at most 6 rows name the same one
- route_gates: float32 [4, 2, 4096, 2], P('section', None, 'expert'), may hold values from 0.1 to 0.6
Outputs:
- input_grads: bfloat16 [4, 2, 4096, 2560], P('section', None, 'expert')
Inputs may be any that keep to these rules, and one draw needn't show every extreme that they name: `route_ids`: each row names 2 different experts. In each aligned block of 64 rows (one device's tokens of one microbatch in one layer) no expert is named by more than 6 rows, and in some block an expert is named by exactly 6 rows.
All inputs are finite; a program needn't handle non-finite values.
Results may differ from a plain program's by a relative error of at most 0.02.
Values may be sent and summed in bfloat16 or wider, within the bound.
A program may use at most 128 MiB of HBM per device.

v0:
```python
import jax
import jax.numpy as jnp
from jax import lax
from jax.sharding import PartitionSpec as P

EPS = 1e-06


def shifted(x, axis, by):
    size = lax.axis_size(axis)
    pairs = [(i, i + by) for i in range(size) if 0 <= i + by < size]
    return lax.ppermute(x, axis, pairs)


def normalize(h_rows, gain_vec):
    widened = h_rows.astype(jnp.float32)
    inv_rms = lax.rsqrt(jnp.mean(widened * widened, axis=-1, keepdims=True) + EPS)
    return (widened * inv_rms * gain_vec).astype(jnp.bfloat16)


def norm_grad(h_rows, gain_vec, upstream):
    widened = h_rows.astype(jnp.float32)
    inv_rms = lax.rsqrt(jnp.mean(widened * widened, axis=-1, keepdims=True) + EPS)
    weighted = gain_vec * upstream
    projected = jnp.mean(widened * weighted, axis=-1, keepdims=True)
    return inv_rms * weighted - widened * inv_rms * inv_rms * inv_rms * projected


def slot_rows(route_rows, route_experts, capacity):
    groups = route_rows.shape[0]
    flattened = route_rows.reshape(groups, -1)
    onehot = (
        flattened[:, :, None] == jnp.arange(route_experts, dtype=jnp.int32)[None, None, :]
    ).astype(jnp.int32)
    before = jnp.cumsum(onehot, axis=1) - onehot
    position = jnp.sum(before * onehot, axis=-1)
    offset = jnp.arange(groups, dtype=jnp.int32)[:, None] * capacity
    return (flattened * (groups * capacity) + offset + position).reshape(-1)


def hand_over(payload, direction):
    return shifted(payload, "section", direction)


def spread_rows(rows, targets, route_experts, slots_each, model_width):
    outgoing = (
        jnp.zeros((route_experts * slots_each, model_width), jnp.bfloat16).at[targets].set(rows)
    )
    outgoing = outgoing.reshape(route_experts, slots_each, model_width)
    return jnp.repeat(outgoing, 2, axis=0)


def gather_halves(returned, targets, route_experts, model_width):
    halves = returned.reshape(route_experts, 2, -1, model_width).astype(jnp.float32)
    combined = (halves[:, 0] + halves[:, 1]).reshape(-1, model_width)
    return combined[targets]


def layer_forward(h_rows, route_rows, gate_rows, gain_vec, weights, active, capacity):
    gate_mat, up_mat, down_mat = weights
    groups, tok_count, model_width = h_rows.shape
    hidden_width = gate_mat.shape[1]
    route_experts = lax.axis_size("expert") // 2
    normed = normalize(h_rows, gain_vec)
    targets = slot_rows(route_rows, route_experts, capacity)
    pairs = jnp.repeat(normed.reshape(-1, model_width), route_rows.shape[-1], axis=0)
    outgoing = spread_rows(pairs, targets, route_experts, groups * capacity, model_width)

    def expert_compute(payload):
        pre_gate = jnp.einsum("ncd,dh->nch", payload, gate_mat, preferred_element_type=jnp.float32)
        pre_up = jnp.einsum("ncd,dh->nch", payload, up_mat, preferred_element_type=jnp.float32)
        hidden = (pre_gate * jax.nn.sigmoid(pre_gate) * pre_up).astype(jnp.bfloat16)
        result = jnp.einsum(
            "nch,hd->ncd", hidden, down_mat, preferred_element_type=jnp.float32
        ).astype(jnp.bfloat16)
        return (result, pre_gate, pre_up)

    def expert_skipped(payload):
        lead, slots_now = (payload.shape[0], payload.shape[1])
        empty = jnp.zeros((lead, slots_now, hidden_width), jnp.float32)
        return (jnp.zeros_like(payload), empty, empty)

    result, pre_gate, pre_up = lax.cond(
        active,
        expert_compute,
        expert_skipped,
        lax.all_to_all(outgoing, "expert", split_axis=0, concat_axis=0, tiled=True),
    )
    returned = lax.all_to_all(result, "expert", split_axis=0, concat_axis=0, tiled=True)
    picked = gather_halves(returned, targets, route_experts, model_width).reshape(
        groups, tok_count, -1, model_width
    )
    mixture = jnp.sum(gate_rows[:, :, :, None] * picked, axis=2)
    return ((h_rows.astype(jnp.float32) + mixture).astype(jnp.bfloat16), pre_gate, pre_up)


def layer_backward(
    h_rows, pre_gate, pre_up, upstream, route_rows, gate_rows, gain_vec, weights, active, capacity
):
    gate_mat, up_mat, down_mat = weights
    groups, tok_count, model_width = h_rows.shape
    route_experts = lax.axis_size("expert") // 2
    targets = slot_rows(route_rows, route_experts, capacity)
    scaled = (gate_rows[:, :, :, None] * upstream[:, :, None, :].astype(jnp.float32)).astype(
        jnp.bfloat16
    )
    outgoing = spread_rows(
        scaled.reshape(-1, model_width), targets, route_experts, groups * capacity, model_width
    )
    arrived = lax.all_to_all(outgoing, "expert", split_axis=0, concat_axis=0, tiled=True)

    def layer_compute(operands):
        payload, gate_pre, up_pre = operands
        grad_hidden = jnp.einsum(
            "ncd,hd->nch", payload, down_mat, preferred_element_type=jnp.float32
        )
        logistic = jax.nn.sigmoid(gate_pre)
        grad_gate = (grad_hidden * up_pre * logistic * (1.0 + gate_pre * (1.0 - logistic))).astype(
            jnp.bfloat16
        )
        grad_up = (grad_hidden * gate_pre * logistic).astype(jnp.bfloat16)
        summed = jnp.einsum(
            "nch,dh->ncd", grad_gate, gate_mat, preferred_element_type=jnp.float32
        ) + jnp.einsum("nch,dh->ncd", grad_up, up_mat, preferred_element_type=jnp.float32)
        return summed.astype(jnp.bfloat16)

    def layer_skipped(operands):
        return jnp.zeros_like(operands[0])

    grad_normed = lax.cond(active, layer_compute, layer_skipped, (arrived, pre_gate, pre_up))
    returned = lax.all_to_all(grad_normed, "expert", split_axis=0, concat_axis=0, tiled=True)
    picked = gather_halves(returned, targets, route_experts, model_width).reshape(
        groups, tok_count, -1, model_width
    )
    summed = jnp.sum(picked, axis=2)
    return (upstream.astype(jnp.float32) + norm_grad(h_rows, gain_vec, summed)).astype(jnp.bfloat16)


def body(tokens, norm_gain, w_gate, w_up, w_down, route_ids, route_gates):
    sections = lax.axis_size("section")
    section_idx = lax.axis_index("section")
    senders = lax.axis_size("expert")
    route_experts = senders // 2
    micro_count, tok_count, model_width = tokens.shape
    top_count = route_ids.shape[-1]
    hidden_width = w_gate.shape[-1]
    capacity = max(2, (4 * tok_count * top_count + 3 * route_experts - 1) // (3 * route_experts))
    gain_vec = norm_gain[0]
    weights = (w_gate[0], w_up[0], w_down[0])
    routes_here = route_ids[0]
    gates_here = route_gates[0]
    groups = 1
    rounds = sections + micro_count // groups - 1
    saved_in = jnp.zeros((micro_count, tok_count, model_width), jnp.bfloat16)
    layer_out = jnp.zeros((micro_count, tok_count, model_width), jnp.bfloat16)
    saved_gate = jnp.zeros((micro_count, senders, capacity, hidden_width), jnp.float32)
    saved_up = jnp.zeros((micro_count, senders, capacity, hidden_width), jnp.float32)
    carried = jnp.zeros((groups, tok_count, model_width), jnp.bfloat16)
    for tick_index in range(rounds):
        if tick_index > 0:
            carried = hand_over(carried, 1)
        first = (tick_index - section_idx) * groups
        active = (first >= 0) & (first < micro_count)
        start = jnp.clip(first, 0, micro_count - groups)
        own_rows = lax.dynamic_slice_in_dim(tokens, start, groups, 0)
        h_rows = jnp.where(section_idx == 0, own_rows, carried)
        route_rows = lax.dynamic_slice_in_dim(routes_here, start, groups, 0)
        gate_rows = lax.dynamic_slice_in_dim(gates_here, start, groups, 0)
        h_next, pre_gate, pre_up = layer_forward(
            h_rows, route_rows, gate_rows, gain_vec, weights, active, capacity
        )
        pre_gate = pre_gate.reshape(senders, groups, capacity, hidden_width).transpose(1, 0, 2, 3)
        pre_up = pre_up.reshape(senders, groups, capacity, hidden_width).transpose(1, 0, 2, 3)
        saved_in = jnp.where(
            active, lax.dynamic_update_slice_in_dim(saved_in, h_rows, start, 0), saved_in
        )
        layer_out = jnp.where(
            active, lax.dynamic_update_slice_in_dim(layer_out, h_next, start, 0), layer_out
        )
        saved_gate = jnp.where(
            active, lax.dynamic_update_slice_in_dim(saved_gate, pre_gate, start, 0), saved_gate
        )
        saved_up = jnp.where(
            active, lax.dynamic_update_slice_in_dim(saved_up, pre_up, start, 0), saved_up
        )
        carried = h_next
    grad_out = jnp.zeros((micro_count, tok_count, model_width), jnp.bfloat16)
    carried = jnp.zeros((groups, tok_count, model_width), jnp.bfloat16)
    for tick_index in range(rounds):
        if tick_index > 0:
            carried = hand_over(carried, -1)
        first = (tick_index - (sections - 1 - section_idx)) * groups
        active = (first >= 0) & (first < micro_count)
        start = jnp.clip(first, 0, micro_count - groups)
        given = lax.dynamic_slice_in_dim(layer_out, start, groups, 0)
        upstream = jnp.where(section_idx == sections - 1, given, carried)
        h_rows = lax.dynamic_slice_in_dim(saved_in, start, groups, 0)
        pre_gate = (
            lax.dynamic_slice_in_dim(saved_gate, start, groups, 0)
            .transpose(1, 0, 2, 3)
            .reshape(senders, groups * capacity, hidden_width)
        )
        pre_up = (
            lax.dynamic_slice_in_dim(saved_up, start, groups, 0)
            .transpose(1, 0, 2, 3)
            .reshape(senders, groups * capacity, hidden_width)
        )
        route_rows = lax.dynamic_slice_in_dim(routes_here, start, groups, 0)
        gate_rows = lax.dynamic_slice_in_dim(gates_here, start, groups, 0)
        grad_in = layer_backward(
            h_rows,
            pre_gate,
            pre_up,
            upstream,
            route_rows,
            gate_rows,
            gain_vec,
            weights,
            active,
            capacity,
        )
        grad_out = jnp.where(
            active, lax.dynamic_update_slice_in_dim(grad_out, grad_in, start, 0), grad_out
        )
        carried = grad_in
    return grad_out[None]


def solution(mesh):
    in_specs = (
        P(None, "expert", None),
        P("section", None),
        P("section", None, "expert"),
        P("section", None, "expert"),
        P("section", "expert", None),
        P("section", None, "expert", None),
        P("section", None, "expert", None),
    )
    out_specs = P("section", None, "expert", None)
    return jax.shard_map(body, mesh=mesh, in_specs=in_specs, out_specs=out_specs, check_vma=False)
```

profile of v0, /device:TPU:1, one launch (start us, length us, event | category | flops | bytes accessed | tf_op | source)
XLA Modules:
  0.0 1826.8 jit_solution(16054962681653368461)
XLA Ops:
  11.0 13.4 all-to-all-start
  24.5 62.2 %all-to-all-done = bf16[64,6,2560]{2,1,0:T(8,128)(2,1)} async-done(((bf16[64,6,2560]{2,1,0:T(8,128)(2,1)}), bf16[64,6,2560]{2,1,0:T(8,128)(2,1)}, u32[]{:S(2)}, u32[]{:S(2)}) %all-to-all-start) | async-done | bytes 1966112 | tf_op jit(solution)/shard_map/all_to_all | solution.py:87
  86.6 11.6 conditional.10
  98.2 4.1 copy.122
  102.4 6.2 all-to-all-start.1
  109.3 61.4 %all-to-all-done.1 = bf16[64,6,2560]{2,1,0:T(8,128)(2,1)S(1)} async-done(((bf16[64,6,2560]{2,1,0:T(8,128)(2,1)}), bf16[64,6,2560]{2,1,0:T(8,128)(2,1)S(1)}, u32[]{:S(2)}, u32[]{:S(2)}) %all-to-all-start.1) | async-done | bytes 1966112 | tf_op jit(solution)/shard_map/all_to_all | solution.py:89
  180.4 7.2 collective-permute-done
  194.9 5.6 all-to-all-start.2
  200.6 62.2 %all-to-all-done.2 = bf16[64,6,2560]{2,1,0:T(8,128)(2,1)} async-done(((bf16[64,6,2560]{2,1,0:T(8,128)(2,1)}), bf16[64,6,2560]{2,1,0:T(8,128)(2,1)}, u32[]{:S(2)}, u32[]{:S(2)}) %all-to-all-start.2) | async-done | bytes 1966112 | tf_op jit(solution)/shard_map/all_to_all | solution.py:87
  262.8 11.9 conditional.11
  274.7 4.1 copy.129
  278.8 6.1 all-to-all-start.3
  286.7 60.4 %all-to-all-done.3 = bf16[64,6,2560]{2,1,0:T(8,128)(2,1)} async-done(((bf16[64,6,2560]{2,1,0:T(8,128)(2,1)}), bf16[64,6,2560]{2,1,0:T(8,128)(2,1)}, u32[]{:S(2)}, u32[]{:S(2)}) %all-to-all-start.3) | async-done | bytes 1966112 | tf_op jit(solution)/shard_map/all_to_all | solution.py:89
  363.8 6.9 collective-permute-done.1
  378.0 6.3 all-to-all-start.4
  384.4 62.2 %all-to-all-done.4 = bf16[64,6,2560]{2,1,0:T(8,128)(2,1)} async-done(((bf16[64,6,2560]{2,1,0:T(8,128)(2,1)}), bf16[64,6,2560]{2,1,0:T(8,128)(2,1)}, u32[]{:S(2)}, u32[]{:S(2)}) %all-to-all-start.4) | async-done | bytes 1966112 | tf_op jit(solution)/shard_map/all_to_all | solution.py:87
  450.1 4.1 copy.136
  454.2 6.0 all-to-all-start.5
  460.4 62.1 %all-to-all-done.5 = bf16[64,6,2560]{2,1,0:T(8,128)(2,1)} async-done(((bf16[64,6,2560]{2,1,0:T(8,128)(2,1)}), bf16[64,6,2560]{2,1,0:T(8,128)(2,1)}, u32[]{:S(2)}, u32[]{:S(2)}) %all-to-all-start.5) | async-done | bytes 1966112 | tf_op jit(solution)/shard_map/all_to_all | solution.py:89
  534.8 12.5 collective-permute-start.2
  547.3 7.1 collective-permute-done.2
  561.9 6.3 all-to-all-start.6
  568.2 62.2 %all-to-all-done.6 = bf16[64,6,2560]{2,1,0:T(8,128)(2,1)} async-done(((bf16[64,6,2560]{2,1,0:T(8,128)(2,1)}), bf16[64,6,2560]{2,1,0:T(8,128)(2,1)}, u32[]{:S(2)}, u32[]{:S(2)}) %all-to-all-start.6) | async-done | bytes 1966112 | tf_op jit(solution)/shard_map/all_to_all | solution.py:87
  633.6 4.1 copy.143
  637.8 5.9 all-to-all-start.7
  645.5 60.4 %all-to-all-done.7 = bf16[64,6,2560]{2,1,0:T(8,128)(2,1)} async-done(((bf16[64,6,2560]{2,1,0:T(8,128)(2,1)}), bf16[64,6,2560]{2,1,0:T(8,128)(2,1)}, u32[]{:S(2)}, u32[]{:S(2)}) %all-to-all-start.7) | async-done | bytes 1966112 | tf_op jit(solution)/shard_map/all_to_all | solution.py:89
  718.2 4.3 collective-permute-start.3
  722.7 6.7 collective-permute-done.3
  736.7 6.3 all-to-all-start.8
  743.1 62.2 %all-to-all-done.8 = bf16[64,6,2560]{2,1,0:T(8,128)(2,1)} async-done(((bf16[64,6,2560]{2,1,0:T(8,128)(2,1)}), bf16[64,6,2560]{2,1,0:T(8,128)(2,1)}, u32[]{:S(2)}, u32[]{:S(2)}) %all-to-all-start.8) | async-done | bytes 1966112 | tf_op jit(solution)/shard_map/all_to_all | solution.py:87
  808.4 4.1 copy.150
  812.5 6.3 all-to-all-start.9
  819.1 61.7 %all-to-all-done.9 = bf16[64,6,2560]{2,1,0:T(8,128)(2,1)S(1)} async-done(((bf16[64,6,2560]{2,1,0:T(8,128)(2,1)}), bf16[64,6,2560]{2,1,0:T(8,128)(2,1)S(1)}, u32[]{:S(2)}, u32[]{:S(2)}) %all-to-all-start.9) | async-done | bytes 1966112 | tf_op jit(solution)/shard_map/all_to_all | solution.py:89
  896.9 5.9 all-to-all-start.10
  916.8 48.2 %all-to-all-done.10 = bf16[64,6,2560]{2,1,0:T(8,128)(2,1)} async-done(((bf16[64,6,2560]{2,1,0:T(8,128)(2,1)}), bf16[64,6,2560]{2,1,0:T(8,128)(2,1)}, u32[]{:S(2)}, u32[]{:S(2)}) %all-to-all-start.10) | async-done | bytes 1966112 | tf_op jit(solution)/shard_map/all_to_all | solution.py:110
  966.6 4.1 copy.157
  970.7 5.9 all-to-all-start.11
  978.6 60.3 %all-to-all-done.11 = bf16[64,6,2560]{2,1,0:T(8,128)(2,1)} async-done(((bf16[64,6,2560]{2,1,0:T(8,128)(2,1)}), bf16[64,6,2560]{2,1,0:T(8,128)(2,1)}, u32[]{:S(2)}, u32[]{:S(2)}) %all-to-all-start.11) | async-done | bytes 1966112 | tf_op jit(solution)/shard_map/all_to_all | solution.py:131
  1057.0 16.4 collective-permute-done.4
  1081.9 5.6 all-to-all-start.12
  1087.5 62.2 %all-to-all-done.12 = bf16[64,6,2560]{2,1,0:T(8,128)(2,1)} async-done(((bf16[64,6,2560]{2,1,0:T(8,128)(2,1)}), bf16[64,6,2560]{2,1,0:T(8,128)(2,1)}, u32[]{:S(2)}, u32[]{:S(2)}) %all-to-all-start.12) | async-done | bytes 1966112 | tf_op jit(solution)/shard_map/all_to_all | solution.py:110
  1151.2 4.1 copy.164
  1155.3 6.5 all-to-all-start.13
  1161.9 62.0 %all-to-all-done.13 = bf16[64,6,2560]{2,1,0:T(8,128)(2,1)} async-done(((bf16[64,6,2560]{2,1,0:T(8,128)(2,1)}), bf16[64,6,2560]{2,1,0:T(8,128)(2,1)}, u32[]{:S(2)}, u32[]{:S(2)}) %all-to-all-start.13) | async-done | bytes 1966112 | tf_op jit(solution)/shard_map/all_to_all | solution.py:131
  1244.1 10.9 collective-permute-done.5
  1264.5 5.7 all-to-all-start.14
  1270.2 62.2 %all-to-all-done.14 = bf16[64,6,2560]{2,1,0:T(8,128)(2,1)} async-done(((bf16[64,6,2560]{2,1,0:T(8,128)(2,1)}), bf16[64,6,2560]{2,1,0:T(8,128)(2,1)}, u32[]{:S(2)}, u32[]{:S(2)}) %all-to-all-start.14) | async-done | bytes 1966112 | tf_op jit(solution)/shard_map/all_to_all | solution.py:110
  1333.9 4.1 copy.171
  1338.1 5.9 all-to-all-start.15
  1348.8 57.4 %all-to-all-done.15 = bf16[64,6,2560]{2,1,0:T(8,128)(2,1)} async-done(((bf16[64,6,2560]{2,1,0:T(8,128)(2,1)}), bf16[64,6,2560]{2,1,0:T(8,128)(2,1)}, u32[]{:S(2)}, u32[]{:S(2)}) %all-to-all-start.15) | async-done | bytes 1966112 | tf_op jit(solution)/shard_map/all_to_all | solution.py:131
  1425.9 37.3 %collective-permute-done.6 = bf16[1,64,2560]{2,1,0:T(8,128)(2,1)S(1)} collective-permute-done((bf16[1,64,2560]{2,1,0:T(8,128)(2,1)S(1)}, bf16[1,64,2560]{2,1,0:T(8,128)(2,1)S(1)}, u32[]{:S(2)}, u32[]{:S(2)}) %collective-permute-start.6) | collective-permute-done | bytes 327712 | tf_op jit(solution)/shard_map/ppermute | solution.py:12
  1472.7 5.6 all-to-all-start.16
  1478.3 62.2 %all-to-all-done.16 = bf16[64,6,2560]{2,1,0:T(8,128)(2,1)} async-done(((bf16[64,6,2560]{2,1,0:T(8,128)(2,1)}), bf16[64,6,2560]{2,1,0:T(8,128)(2,1)}, u32[]{:S(2)}, u32[]{:S(2)}) %all-to-all-start.16) | async-done | bytes 1966112 | tf_op jit(solution)/shard_map/all_to_all | solution.py:110
  1540.6 8.6 conditional.18
  1549.1 4.1 copy.178
  1553.3 6.7 all-to-all-start.17
  1560.0 61.9 %all-to-all-done.17 = bf16[64,6,2560]{2,1,0:T(8,128)(2,1)} async-done(((bf16[64,6,2560]{2,1,0:T(8,128)(2,1)}), bf16[64,6,2560]{2,1,0:T(8,128)(2,1)}, u32[]{:S(2)}, u32[]{:S(2)}) %all-to-all-start.17) | async-done | bytes 1966112 | tf_op jit(solution)/shard_map/all_to_all | solution.py:131
  1642.1 10.3 collective-permute-done.7
  1662.0 5.8 all-to-all-start.18
  1667.8 62.2 %all-to-all-done.18 = bf16[64,6,2560]{2,1,0:T(8,128)(2,1)} async-done(((bf16[64,6,2560]{2,1,0:T(8,128)(2,1)}), bf16[64,6,2560]{2,1,0:T(8,128)(2,1)}, u32[]{:S(2)}, u32[]{:S(2)}) %all-to-all-start.18) | async-done | bytes 1966112 | tf_op jit(solution)/shard_map/all_to_all | solution.py:110
  1730.0 8.8 conditional.19
  1738.7 4.1 copy.185
  1742.9 6.0 all-to-all-start.19
  1749.8 61.3 %all-to-all-done.19 = bf16[64,6,2560]{2,1,0:T(8,128)(2,1)} async-done(((bf16[64,6,2560]{2,1,0:T(8,128)(2,1)}), bf16[64,6,2560]{2,1,0:T(8,128)(2,1)}, u32[]{:S(2)}, u32[]{:S(2)}) %all-to-all-start.19) | async-done | bytes 1966112 | tf_op jit(solution)/shard_map/all_to_all | solution.py:131
  (477 shorter events, 332.5 us)
Async XLA Ops:
  7.0 182.2 %copy-start.76 = (s32[128]{0:T(128)}, s32[128]{0:T(128)S(1)}, u32[]{:S(2)}) copy-start(s32[128]{0:T(128)S(1)} %get-tuple-element.552) | copy-start | bytes 1540
  11.0 75.6 %copy-start.6 = (bf16[1,2560,384]{2,1,0:T(8,128)(2,1)S(1)}, bf16[1,2560,384]{2,1,0:T(8,128)(2,1)}, u32[]{:S(2)}) copy-start(bf16[1,2560,384]{2,1,0:T(8,128)(2,1)} %param.30) | copy-start | bytes 5898244
  11.0 75.6 %all-to-all-start = ((bf16[64,6,2560]{2,1,0:T(8,128)(2,1)}), bf16[64,6,2560]{2,1,0:T(8,128)(2,1)}, u32[]{:S(2)}, u32[]{:S(2)}) async-start(bf16[64,6,2560]{2,1,0:T(8,128)(2,1)} %bitcast.620), calls=%async_computation | async-start | bytes 5242880 | tf_op jit(solution)/shard_map/all_to_all | solution.py:87
  102.4 68.3 %all-to-all-start.1 = ((bf16[64,6,2560]{2,1,0:T(8,128)(2,1)}), bf16[64,6,2560]{2,1,0:T(8,128)(2,1)S(1)}, u32[]{:S(2)}, u32[]{:S(2)}) async-start(bf16[64,6,2560]{2,1,0:T(8,128)(2,1)} %copy.122), calls=%async_computation.1 | async-start | bytes 5242880 | tf_op jit(solution)/shard_map/all_to_all | solution.py:89
  178.9 8.7 collective-permute-start
  194.9 67.8 %copy-start.7 = (bf16[1,2560,384]{2,1,0:T(8,128)(2,1)S(1)}, bf16[1,2560,384]{2,1,0:T(8,128)(2,1)}, u32[]{:S(2)}) copy-start(bf16[1,2560,384]{2,1,0:T(8,128)(2,1)} %param.30) | copy-start | bytes 5898244
  194.9 67.8 %all-to-all-start.2 = ((bf16[64,6,2560]{2,1,0:T(8,128)(2,1)}), bf16[64,6,2560]{2,1,0:T(8,128)(2,1)}, u32[]{:S(2)}, u32[]{:S(2)}) async-start(bf16[64,6,2560]{2,1,0:T(8,128)(2,1)} %bitcast.624), calls=%async_computation.2 | async-start | bytes 5242880 | tf_op jit(solution)/shard_map/all_to_all | solution.py:87
  278.8 7.2 copy-start.70
  278.8 7.5 copy-start.68
  278.8 7.7 copy-start.77
  278.8 68.3 %all-to-all-start.3 = ((bf16[64,6,2560]{2,1,0:T(8,128)(2,1)}), bf16[64,6,2560]{2,1,0:T(8,128)(2,1)}, u32[]{:S(2)}, u32[]{:S(2)}) async-start(bf16[64,6,2560]{2,1,0:T(8,128)(2,1)} %copy.129), calls=%async_computation.3 | async-start | bytes 5242880 | tf_op jit(solution)/shard_map/all_to_all | solution.py:89
  357.5 13.2 copy-start.41
  359.5 11.2 collective-permute-start.1
  363.8 192.2 %copy-start.74 = (s32[128]{0:T(128)}, s32[128]{0:T(128)S(1)}, u32[]{:S(2)}) copy-start(s32[128]{0:T(128)S(1)} %get-tuple-element.554) | copy-start | bytes 1540
  378.0 68.5 %copy-start.8 = (bf16[1,2560,384]{2,1,0:T(8,128)(2,1)S(1)}, bf16[1,2560,384]{2,1,0:T(8,128)(2,1)}, u32[]{:S(2)}) copy-start(bf16[1,2560,384]{2,1,0:T(8,128)(2,1)} %param.30) | copy-start | bytes 5898244
  378.0 68.5 %all-to-all-start.4 = ((bf16[64,6,2560]{2,1,0:T(8,128)(2,1)}), bf16[64,6,2560]{2,1,0:T(8,128)(2,1)}, u32[]{:S(2)}, u32[]{:S(2)}) async-start(bf16[64,6,2560]{2,1,0:T(8,128)(2,1)} %bitcast.625), calls=%async_computation.4 | async-start | bytes 5242880 | tf_op jit(solution)/shard_map/all_to_all | solution.py:87
  454.2 68.2 %all-to-all-start.5 = ((bf16[64,6,2560]{2,1,0:T(8,128)(2,1)}), bf16[64,6,2560]{2,1,0:T(8,128)(2,1)}, u32[]{:S(2)}, u32[]{:S(2)}) async-start(bf16[64,6,2560]{2,1,0:T(8,128)(2,1)} %copy.136), calls=%async_computation.5 | async-start | bytes 5242880 | tf_op jit(solution)/shard_map/all_to_all | solution.py:89
  532.8 21.6 %copy-start.42 = (bf16[2,64,2560]{2,1,0:T(8,128)(2,1)S(1)}, bf16[2,64,2560]{2,1,0:T(8,128)(2,1)}, u32[]{:S(2)}) copy-start(bf16[2,64,2560]{2,1,0:T(8,128)(2,1)} %param.27) | copy-start | bytes 1966084
  534.8 19.6 %collective-permute-start.2 = (bf16[1,64,2560]{2,1,0:T(8,128)(2,1)S(1)}, bf16[1,64,2560]{2,1,0:T(8,128)(2,1)S(1)}, u32[]{:S(2)}, u32[]{:S(2)}) collective-permute-start(bf16[1,64,2560]{2,1,0:T(8,128)(2,1)S(1)} %get-tuple-element.510), channel_id=1, source_target_pairs={{0,64},{64,128},{128,192},{1,65},{65,129},{129,193},{2,66},{66,130... | collective-permute-start | bytes 983048 | tf_op jit(solution)/shard_map/ppermute | solution.py:12
  561.9 68.5 %copy-start.9 = (bf16[1,2560,384]{2,1,0:T(8,128)(2,1)S(1)}, bf16[1,2560,384]{2,1,0:T(8,128)(2,1)}, u32[]{:S(2)}) copy-start(bf16[1,2560,384]{2,1,0:T(8,128)(2,1)} %param.30) | copy-start | bytes 5898244
  561.9 68.5 %all-to-all-start.6 = ((bf16[64,6,2560]{2,1,0:T(8,128)(2,1)}), bf16[64,6,2560]{2,1,0:T(8,128)(2,1)}, u32[]{:S(2)}, u32[]{:S(2)}) async-start(bf16[64,6,2560]{2,1,0:T(8,128)(2,1)} %bitcast.626), calls=%async_computation.6 | async-start | bytes 5242880 | tf_op jit(solution)/shard_map/all_to_all | solution.py:87
  637.7 6.6 copy-start.65
  637.7 7.1 copy-start.64
  637.7 7.5 copy-start.75
  637.8 68.1 %all-to-all-start.7 = ((bf16[64,6,2560]{2,1,0:T(8,128)(2,1)}), bf16[64,6,2560]{2,1,0:T(8,128)(2,1)}, u32[]{:S(2)}, u32[]{:S(2)}) async-start(bf16[64,6,2560]{2,1,0:T(8,128)(2,1)} %copy.143), calls=%async_computation.7 | async-start | bytes 5242880 | tf_op jit(solution)/shard_map/all_to_all | solution.py:89
  716.2 13.2 copy-start.43
  718.2 11.2 collective-permute-start.3
  736.7 68.5 %copy-start.10 = (bf16[1,2560,384]{2,1,0:T(8,128)(2,1)S(1)}, bf16[1,2560,384]{2,1,0:T(8,128)(2,1)}, u32[]{:S(2)}) copy-start(bf16[1,2560,384]{2,1,0:T(8,128)(2,1)} %param.30) | copy-start | bytes 5898244
  736.7 68.5 %all-to-all-start.8 = ((bf16[64,6,2560]{2,1,0:T(8,128)(2,1)}), bf16[64,6,2560]{2,1,0:T(8,128)(2,1)}, u32[]{:S(2)}, u32[]{:S(2)}) async-start(bf16[64,6,2560]{2,1,0:T(8,128)(2,1)} %bitcast.627), calls=%async_computation.8 | async-start | bytes 5242880 | tf_op jit(solution)/shard_map/all_to_all | solution.py:87
  812.5 68.4 %all-to-all-start.9 = ((bf16[64,6,2560]{2,1,0:T(8,128)(2,1)}), bf16[64,6,2560]{2,1,0:T(8,128)(2,1)S(1)}, u32[]{:S(2)}, u32[]{:S(2)}) async-start(bf16[64,6,2560]{2,1,0:T(8,128)(2,1)} %copy.150), calls=%async_computation.9 | async-start | bytes 5242880 | tf_op jit(solution)/shard_map/all_to_all | solution.py:89
  896.9 68.1 %all-to-all-start.10 = ((bf16[64,6,2560]{2,1,0:T(8,128)(2,1)}), bf16[64,6,2560]{2,1,0:T(8,128)(2,1)}, u32[]{:S(2)}, u32[]{:S(2)}) async-start(bf16[64,6,2560]{2,1,0:T(8,128)(2,1)} %bitcast.94), calls=%async_computation.10 | async-start | bytes 5242880 | tf_op jit(solution)/shard_map/all_to_all | solution.py:110
  914.6 50.4 %copy-start.11 = (bf16[1,2560,384]{2,1,0:T(8,128)(2,1)S(1)}, bf16[1,2560,384]{2,1,0:T(8,128)(2,1)}, u32[]{:S(2)}) copy-start(bf16[1,2560,384]{2,1,0:T(8,128)(2,1)} %param.30) | copy-start | bytes 5898244
  970.7 68.1 %all-to-all-start.11 = ((bf16[64,6,2560]{2,1,0:T(8,128)(2,1)}), bf16[64,6,2560]{2,1,0:T(8,128)(2,1)}, u32[]{:S(2)}, u32[]{:S(2)}) async-start(bf16[64,6,2560]{2,1,0:T(8,128)(2,1)} %copy.157), calls=%async_computation.11 | async-start | bytes 5242880 | tf_op jit(solution)/shard_map/all_to_all | solution.py:131
  1055.3 18.1 collective-permute-start.4
  1057.0 201.7 %copy-start.78 = (s32[128]{0:T(128)}, s32[128]{0:T(128)S(1)}, u32[]{:S(2)}) copy-start(s32[128]{0:T(128)S(1)} %get-tuple-element.558) | copy-start | bytes 1540
  1081.9 67.8 %copy-start.12 = (bf16[1,2560,384]{2,1,0:T(8,128)(2,1)S(1)}, bf16[1,2560,384]{2,1,0:T(8,128)(2,1)}, u32[]{:S(2)}) copy-start(bf16[1,2560,384]{2,1,0:T(8,128)(2,1)} %param.30) | copy-start | bytes 5898244
  1081.9 67.8 %all-to-all-start.12 = ((bf16[64,6,2560]{2,1,0:T(8,128)(2,1)}), bf16[64,6,2560]{2,1,0:T(8,128)(2,1)}, u32[]{:S(2)}, u32[]{:S(2)}) async-start(bf16[64,6,2560]{2,1,0:T(8,128)(2,1)} %bitcast.621), calls=%async_computation.12 | async-start | bytes 5242880 | tf_op jit(solution)/shard_map/all_to_all | solution.py:110
  1155.3 68.5 %all-to-all-start.13 = ((bf16[64,6,2560]{2,1,0:T(8,128)(2,1)}), bf16[64,6,2560]{2,1,0:T(8,128)(2,1)}, u32[]{:S(2)}, u32[]{:S(2)}) async-start(bf16[64,6,2560]{2,1,0:T(8,128)(2,1)} %copy.164), calls=%async_computation.13 | async-start | bytes 5242880 | tf_op jit(solution)/shard_map/all_to_all | solution.py:131
  1232.1 6.9 copy-start.2
  1242.5 22.0 %copy-start.34 = (bf16[2,64,2560]{2,1,0:T(8,128)(2,1)}, bf16[2,64,2560]{2,1,0:T(8,128)(2,1)S(1)}, u32[]{:S(2)}) copy-start(bf16[2,64,2560]{2,1,0:T(8,128)(2,1)S(1)} %get-tuple-element.489) | copy-start | bytes 1966084
  1242.5 12.4 collective-permute-start.5
  1264.5 67.9 %copy-start.13 = (bf16[1,2560,384]{2,1,0:T(8,128)(2,1)S(1)}, bf16[1,2560,384]{2,1,0:T(8,128)(2,1)}, u32[]{:S(2)}) copy-start(bf16[1,2560,384]{2,1,0:T(8,128)(2,1)} %param.30) | copy-start | bytes 5898244
  1264.5 67.8 %all-to-all-start.14 = ((bf16[64,6,2560]{2,1,0:T(8,128)(2,1)}), bf16[64,6,2560]{2,1,0:T(8,128)(2,1)}, u32[]{:S(2)}, u32[]{:S(2)}) async-start(bf16[64,6,2560]{2,1,0:T(8,128)(2,1)} %bitcast.622), calls=%async_computation.14 | async-start | bytes 5242880 | tf_op jit(solution)/shard_map/all_to_all | solution.py:110
  1338.1 6.5 copy-start.60
  1338.1 7.0 copy-start.59
  1338.1 7.8 copy-start.58
  1338.1 8.6 copy-start.62
  1338.1 9.4 copy-start.79
  1338.1 10.2 copy-start.83
  1338.1 68.1 %all-to-all-start.15 = ((bf16[64,6,2560]{2,1,0:T(8,128)(2,1)}), bf16[64,6,2560]{2,1,0:T(8,128)(2,1)}, u32[]{:S(2)}, u32[]{:S(2)}) async-start(bf16[64,6,2560]{2,1,0:T(8,128)(2,1)} %copy.171), calls=%async_computation.15 | async-start | bytes 5242880 | tf_op jit(solution)/shard_map/all_to_all | solution.py:131
  1344.8 63.8 %copy-start.55 = (s32[128]{0:T(128)}, s32[128]{0:T(128)S(1)}, u32[]{:S(2)}) copy-start(s32[128]{0:T(128)S(1)} %eq.318) | copy-start | bytes 1540
  1414.5 6.9 copy-start.3
  1424.2 48.6 %copy-start.36 = (bf16[2,64,2560]{2,1,0:T(8,128)(2,1)}, bf16[2,64,2560]{2,1,0:T(8,128)(2,1)S(1)}, u32[]{:S(2)}) copy-start(bf16[2,64,2560]{2,1,0:T(8,128)(2,1)S(1)} %get-tuple-element.485) | copy-start | bytes 1966084
  1424.2 39.0 %collective-permute-start.6 = (bf16[1,64,2560]{2,1,0:T(8,128)(2,1)S(1)}, bf16[1,64,2560]{2,1,0:T(8,128)(2,1)S(1)}, u32[]{:S(2)}, u32[]{:S(2)}) collective-permute-start(bf16[1,64,2560]{2,1,0:T(8,128)(2,1)S(1)} %get-tuple-element.486), channel_id=1, source_target_pairs={{64,0},{128,64},{192,128},{65,1},{129,65},{193,129},{66,2},{130,66... | collective-permute-start | bytes 983048 | tf_op jit(solution)/shard_map/ppermute | solution.py:12
  1472.7 67.8 %copy-start.14 = (bf16[1,2560,384]{2,1,0:T(8,128)(2,1)S(1)}, bf16[1,2560,384]{2,1,0:T(8,128)(2,1)}, u32[]{:S(2)}) copy-start(bf16[1,2560,384]{2,1,0:T(8,128)(2,1)} %param.30) | copy-start | bytes 5898244
  1472.7 67.8 %all-to-all-start.16 = ((bf16[64,6,2560]{2,1,0:T(8,128)(2,1)}), bf16[64,6,2560]{2,1,0:T(8,128)(2,1)}, u32[]{:S(2)}, u32[]{:S(2)}) async-start(bf16[64,6,2560]{2,1,0:T(8,128)(2,1)} %bitcast.623), calls=%async_computation.16 | async-start | bytes 5242880 | tf_op jit(solution)/shard_map/all_to_all | solution.py:110
  1553.3 6.7 copy-start.82
  1553.3 68.7 %all-to-all-start.17 = ((bf16[64,6,2560]{2,1,0:T(8,128)(2,1)}), bf16[64,6,2560]{2,1,0:T(8,128)(2,1)}, u32[]{:S(2)}, u32[]{:S(2)}) async-start(bf16[64,6,2560]{2,1,0:T(8,128)(2,1)} %copy.178), calls=%async_computation.17 | async-start | bytes 5242880 | tf_op jit(solution)/shard_map/all_to_all | solution.py:131
  1630.2 6.9 copy-start.4
  1640.6 21.4 %copy-start.38 = (bf16[2,64,2560]{2,1,0:T(8,128)(2,1)}, bf16[2,64,2560]{2,1,0:T(8,128)(2,1)S(1)}, u32[]{:S(2)}) copy-start(bf16[2,64,2560]{2,1,0:T(8,128)(2,1)S(1)} %get-tuple-element.481) | copy-start | bytes 1966084
  1640.6 11.9 collective-permute-start.7
  1662.0 68.0 %copy-start.15 = (bf16[1,2560,384]{2,1,0:T(8,128)(2,1)S(1)}, bf16[1,2560,384]{2,1,0:T(8,128)(2,1)}, u32[]{:S(2)}) copy-start(bf16[1,2560,384]{2,1,0:T(8,128)(2,1)} %param.30) | copy-start | bytes 5898244
  1662.0 68.0 %all-to-all-start.18 = ((bf16[64,6,2560]{2,1,0:T(8,128)(2,1)}), bf16[64,6,2560]{2,1,0:T(8,128)(2,1)}, u32[]{:S(2)}, u32[]{:S(2)}) async-start(bf16[64,6,2560]{2,1,0:T(8,128)(2,1)} %bitcast.619), calls=%async_computation.18 | async-start | bytes 5242880 | tf_op jit(solution)/shard_map/all_to_all | solution.py:110
  1742.9 68.2 %all-to-all-start.19 = ((bf16[64,6,2560]{2,1,0:T(8,128)(2,1)}), bf16[64,6,2560]{2,1,0:T(8,128)(2,1)}, u32[]{:S(2)}, u32[]{:S(2)}) async-start(bf16[64,6,2560]{2,1,0:T(8,128)(2,1)} %copy.185), calls=%async_computation.19 | async-start | bytes 5242880 | tf_op jit(solution)/shard_map/all_to_all | solution.py:131
  (45 other events, 179.7 us)
where the time goes:
time: 1840 us; the launch traced here: 1830 us
  waiting for transfers between devices  1320 us (72%)
  local copies, waits for them, and re-layouts  193 us (10%)
  starting transfers between devices  156 us (8%)
  other arithmetic  115 us (6%)
  matrix products  40.4 us (2%)
    all_to_all x5, waiting for transfers between devices, layer_forward(): lax.all_to_all(outgoing, 'expert', split_axis=0, concat_axis=0, tiled=True)  311 us
    all_to_all x5, waiting for transfers between devices, layer_forward(): lax.all_to_all(result, 'expert', split_axis=0, concat_axis=0, tiled=True)  306 us
    all_to_all x5, waiting for transfers between devices, layer_backward(): lax.all_to_all(grad_normed, 'expert', split_axis=0, concat_axis=0, tiled=...  303 us
    all_to_all x5, waiting for transfers between devices, layer_backward(): lax.all_to_all(outgoing, 'expert', split_axis=0, concat_axis=0, tiled=True)  297 us
    ppermute x8, waiting for transfers between devices, shifted(): return lax.ppermute(x, axis, pairs)  103 us
    all_to_all x5, starting transfers between devices, layer_forward(): lax.all_to_all(outgoing, 'expert', split_axis=0, concat_axis=0, tiled=True)  38 us
  transfers between devices with their start and end apart: 28, of which 28 were waited for; matrix products, arithmetic and copies ran while one was open for 1% of the time, Pallas kernels for 0%

commit v1 on v0

v1 whole, which is shorter than its diff:
```python
import functools

import jax
import jax.numpy as jnp
from jax import lax
from jax.experimental import pallas as pl
from jax.experimental.pallas import tpu as pltpu
from jax.sharding import PartitionSpec as P

EPS = 1e-06
PARTS = 4
MESH = pl.DeviceIdType.MESH
F32 = jnp.float32
BF16 = jnp.bfloat16


def mm(a, b):
    return jnp.dot(a, b, preferred_element_type=F32)


def mm_nt(a, b):
    return lax.dot_general(a, b, (((1,), (1,)), ((), ())), preferred_element_type=F32)


def kernel(
    dims,
    tokens_ref,
    gain_ref,
    route_row_ref,
    route_col_ref,
    gate_col_ref,
    perm_ref,
    perm_t_ref,
    w_gate_ref,
    w_up_ref,
    w_down_ref,
    out_ref,
    wg,
    wu,
    wd,
    h_in,
    h_out,
    g_in,
    g_out,
    send_a,
    recv_a,
    send_b,
    recv_b,
    spread,
    collect,
    stage,
    pieces,
    rows,
    pre_g,
    pre_u,
    act_a,
    act_b,
    w_local,
    w_send,
    w_recv,
    a_send,
    a_recv,
    b_send,
    b_recv,
    x_send,
    x_recv,
):
    sections, chips, cap, tok, width, micro, groups, half = dims
    blk = PARTS * cap
    part = width // PARTS
    per = chips // groups
    grp_rows = per * cap
    all_rows = chips * cap
    hidden = 2 * half
    step = 256
    s = lax.axis_index("section")
    ex = lax.axis_index("expert")
    core = lax.rem(ex, 2)
    chip = lax.div(ex, 2)
    mate = 2 * chip + (1 - core)
    my_group = lax.div(chip, per)

    def other(j):
        return lax.rem(chip + j, chips)

    barrier = pltpu.get_barrier_semaphore()

    def greet(j, carry):
        pl.semaphore_signal(
            barrier, inc=1, device_id={"expert": 2 * other(j) + core}, device_id_type=MESH
        )
        return carry

    lax.fori_loop(1, chips, greet, 0)
    pl.semaphore_signal(barrier, inc=1, device_id={"expert": mate}, device_id_type=MESH)

    @pl.when(s > 0)
    def _():
        pl.semaphore_signal(barrier, inc=1, device_id={"section": s - 1}, device_id_type=MESH)

    @pl.when(s < sections - 1)
    def _():
        pl.semaphore_signal(barrier, inc=1, device_id={"section": s + 1}, device_id_type=MESH)

    local = [
        pltpu.make_async_copy(w_gate_ref, wg.at[:, :half], w_local.at[0]),
        pltpu.make_async_copy(w_up_ref, wu.at[:, :half], w_local.at[1]),
        pltpu.make_async_copy(w_down_ref, wd.at[:half, :], w_local.at[2]),
    ]
    for copy in local:
        copy.start()

    ahead = lax.convert_element_type(s > 0, jnp.int32)
    behind = lax.convert_element_type(s < sections - 1, jnp.int32)
    pl.semaphore_wait(barrier, chips + ahead + behind)

    remote = [
        pltpu.make_async_remote_copy(
            src, dst, w_send.at[i], w_recv.at[i], device_id={"expert": mate}, device_id_type=MESH
        )
        for i, (src, dst) in enumerate(
            (
                (w_gate_ref, wg.at[:, half:]),
                (w_up_ref, wu.at[:, half:]),
                (w_down_ref, wd.at[half:, :]),
            )
        )
    ]
    for copy in remote:
        copy.start()

    for m in range(micro):
        for k in range(2):
            at = k * PARTS * tok
            n = PARTS * tok
            lane = route_row_ref[m, :, at : at + n]
            ids = lax.broadcasted_iota(jnp.int32, (chips * blk, n), 0)
            spread[m, :, at : at + n] = jnp.where(ids == lane, 1.0, 0.0).astype(BF16)
            sub = route_col_ref[m, at : at + n, :]
            ids = lax.broadcasted_iota(jnp.int32, (n, chips * blk), 1)
            collect[m, at : at + n, :] = jnp.where(ids == sub, 1.0, 0.0).astype(BF16)

    def send_block(u, d, src, dst, send_sem, recv_sem):
        return pltpu.make_async_remote_copy(
            src.at[u, d],
            dst.at[u, chip],
            send_sem.at[u],
            recv_sem.at[u, my_group],
            device_id={"expert": 2 * d + core},
            device_id_type=MESH,
        )

    def scatter(u, src, dst, send_sem, recv_sem):
        def one(j, carry):
            send_block(u, other(j), src, dst, send_sem, recv_sem).start()
            return carry

        lax.fori_loop(1, chips, one, 0)
        pltpu.make_async_copy(src.at[u, chip], dst.at[u, chip], recv_sem.at[u, my_group]).start()

    def group_wait(u, g, dst, recv_sem):
        view = dst.at[u, pl.ds(g * per, per)]
        pltpu.make_async_copy(view, view, recv_sem.at[u, g]).wait()

    def arrive(u):
        def one(i, carry):
            g = lax.rem(my_group + i, groups)
            group_wait(u, g, recv_a, a_recv)
            got = recv_a[u, pl.ds(g * per, per)].astype(F32).reshape(per * blk, part).astype(BF16)
            sorted_rows = mm(perm_ref[...], got).astype(BF16)
            for q in range(PARTS):
                rows[pl.ds(g * grp_rows, grp_rows), q * part : (q + 1) * part] = sorted_rows[
                    q * grp_rows : (q + 1) * grp_rows
                ]
            return carry

        lax.fori_loop(0, groups, one, 0)

    def give_back(u):
        def one(g, carry):
            got = mm(perm_t_ref[...], pieces[g])
            send_b[u, pl.ds(g * per, per)] = got.reshape(per, blk, part).astype(BF16)
            return carry

        lax.fori_loop(0, groups, one, 0)
        scatter(u, send_b, recv_b, b_send, b_recv)

    def wait_back(u):
        def one(g, carry):
            group_wait(u, g, recv_b, b_recv)
            return carry

        lax.fori_loop(0, groups, one, 0)
        return recv_b[u].astype(F32).reshape(chips * blk, part).astype(BF16)

    def put_pieces(q, value):
        for g in range(groups):
            pieces[g, pl.ds(q * grp_rows, grp_rows), :] = value[g * grp_rows : (g + 1) * grp_rows]

    def inverse_rms(h):
        total = jnp.sum(jnp.sum(h * h, axis=-1, keepdims=True), axis=0)
        return lax.rsqrt(total / width + EPS)

    def hop(buf_src, buf_dst, m, index, to):
        return pltpu.make_async_remote_copy(
            buf_src.at[m],
            buf_dst.at[m],
            x_send.at[index],
            x_recv.at[index],
            device_id={"section": to},
            device_id_type=MESH,
        )

    def forward(m, carry):
        u = m

        @pl.when(s == 0)
        def _():
            for q in range(PARTS):
                h_in[m, q] = tokens_ref[m, :, q * part : (q + 1) * part]

        @pl.when(s > 0)
        def _():
            hop(h_out, h_in, m, m, s).wait_recv()

        h = h_in[m].astype(F32)
        inv = inverse_rms(h)
        for q in range(PARTS):
            stage[pl.ds(q * tok, tok), :] = (
                h_in[m, q].astype(F32) * inv * gain_ref[:, q * part : (q + 1) * part]
            ).astype(BF16)
        n = PARTS * tok
        sel = spread[m, :, :n] + spread[m, :, n:]
        out = mm(sel, stage[:n, :])
        send_a[u] = out.reshape(chips, blk, part).astype(BF16)
        scatter(u, send_a, recv_a, a_send, a_recv)

        @pl.when(m == 0)
        def _():
            for copy in local:
                copy.wait()
            for copy in remote:
                copy.wait_recv()

        arrive(u)

        def first(i, carry):
            at = pl.ds(pl.multiple_of(i * step, step), step)
            gate = mm(rows[...], wg[:, at])
            up = mm(rows[...], wu[:, at])
            pre_g[m, i] = gate
            pre_u[m, i] = up
            act_a[:, at] = (gate * jax.nn.sigmoid(gate) * up).astype(BF16)
            return carry

        lax.fori_loop(0, hidden // step, first, 0)

        def second(q, carry):
            at = pl.ds(pl.multiple_of(q * part, part), part)
            put_pieces(q, mm(act_a[...], wd[:, at]).astype(BF16))
            return carry

        lax.fori_loop(0, PARTS, second, 0)
        give_back(u)
        back = wait_back(u)
        picked = mm(collect[m], back) * gate_col_ref[m]
        mixture = picked[:n] + picked[n:]
        h_out[m] = (h_in[m].astype(F32) + mixture.reshape(PARTS, tok, part)).astype(BF16)

        @pl.when(s < sections - 1)
        def _():
            hop(h_out, h_in, m, m, s + 1).start()

        return carry

    lax.fori_loop(0, micro, forward, 0)

    def backward(m, carry):
        u = micro + m

        @pl.when(s == sections - 1)
        def _():
            g_in[m] = h_out[m]

        @pl.when(s < sections - 1)
        def _():
            hop(g_out, g_in, m, micro + m, s).wait_recv()

        n = PARTS * tok
        upstream = g_in[m].astype(F32).reshape(n, part)
        stage[:n, :] = (gate_col_ref[m, :n] * upstream).astype(BF16)
        stage[n:, :] = (gate_col_ref[m, n:] * upstream).astype(BF16)
        out = mm(spread[m], stage[...])
        send_a[u] = out.reshape(chips, blk, part).astype(BF16)
        scatter(u, send_a, recv_a, a_send, a_recv)
        arrive(u)

        def first(i, carry):
            at = pl.ds(pl.multiple_of(i * step, step), step)
            grad = mm_nt(rows[...], wd[at, :])
            gate = pre_g[m, i]
            up = pre_u[m, i]
            logistic = jax.nn.sigmoid(gate)
            act_a[:, at] = (grad * up * logistic * (1.0 + gate * (1.0 - logistic))).astype(BF16)
            act_b[:, at] = (grad * gate * logistic).astype(BF16)
            return carry

        lax.fori_loop(0, hidden // step, first, 0)

        def second(q, carry):
            at = pl.ds(pl.multiple_of(q * part, part), part)
            value = mm_nt(act_a[...], wg[at, :]) + mm_nt(act_b[...], wu[at, :])
            put_pieces(q, value.astype(BF16))
            return carry

        lax.fori_loop(0, PARTS, second, 0)
        give_back(u)
        back = wait_back(u)
        sel = collect[m, :n] + collect[m, n:]
        total = mm(sel, back).reshape(PARTS, tok, part)
        h = h_in[m].astype(F32)
        inv = inverse_rms(h)
        gain = jnp.stack([gain_ref[:, q * part : (q + 1) * part] for q in range(PARTS)])
        weighted = total * gain
        dot = jnp.sum(jnp.sum(h * weighted, axis=-1, keepdims=True), axis=0) / width
        grad = inv[None] * weighted - h * (inv * inv * inv * dot)[None]
        g_out[m] = (g_in[m].astype(F32) + grad).astype(BF16)

        @pl.when(s > 0)
        def _():
            hop(g_out, g_in, m, micro + m, s - 1).start()

        for q in range(PARTS):
            out_ref[m, :, q * part : (q + 1) * part] = g_out[m, q]
        return carry

    lax.fori_loop(0, micro, backward, 0)

    for copy in remote:
        copy.wait_send()

    def drain(u, carry):
        for buf, sem in ((send_a, a_send), (send_b, b_send)):
            view = buf.at[u, pl.ds(0, chips - 1)]
            pltpu.make_async_copy(view, view, sem.at[u]).wait()
        return carry

    lax.fori_loop(0, 2 * micro, drain, 0)
    for m in range(micro):

        @pl.when(s < sections - 1)
        def _():
            hop(h_out, h_in, m, m, s).wait_send()

        @pl.when(s > 0)
        def _():
            hop(g_out, g_in, m, micro + m, s).wait_send()


def body(tokens, norm_gain, w_gate, w_up, w_down, route_ids, route_gates):
    sections = lax.axis_size("section")
    chips = lax.axis_size("expert") // 2
    micro, tok, width = tokens.shape
    top = route_ids.shape[-1]
    half = w_gate.shape[-1]
    hidden = 2 * half
    cap = max(2, (4 * tok * top + 3 * chips - 1) // (3 * chips))
    blk = PARTS * cap
    part = width // PARTS
    groups = 4
    per = chips // groups
    grp = per * cap
    units = 2 * micro

    flat = route_ids[0].reshape(micro, tok * top)
    onehot = (flat[:, :, None] == jnp.arange(chips, dtype=jnp.int32)).astype(jnp.int32)
    before = jnp.cumsum(onehot, axis=1) - onehot
    position = jnp.sum(before * onehot, axis=-1)
    first = (flat * blk + position).reshape(micro, tok, top).transpose(0, 2, 1)
    offset = jnp.arange(PARTS, dtype=jnp.int32) * cap
    target = (first[:, :, None, :] + offset[None, None, :, None]).reshape(micro, top * PARTS * tok)
    gates = route_gates[0].transpose(0, 2, 1)
    gates = jnp.broadcast_to(gates[:, :, None, :], (micro, top, PARTS, tok)).reshape(micro, -1, 1)

    src = jnp.arange(per * blk, dtype=jnp.int32)
    dest = (src % blk // cap) * grp + src // blk * cap + src % cap
    perm_t = (dest[:, None] == src[None, :]).astype(BF16)
    perm = (src[:, None] == dest[None, :]).astype(BF16)

    dims = (sections, chips, cap, tok, width, micro, groups, half)
    vmem = pl.BlockSpec(memory_space=pltpu.VMEM)
    hbm = pl.BlockSpec(memory_space=pl.ANY)
    dma = pltpu.SemaphoreType.DMA
    result = pl.pallas_call(
        functools.partial(kernel, dims),
        out_shape=jax.ShapeDtypeStruct((micro, tok, width), BF16),
        in_specs=[vmem] * 7 + [hbm] * 3,
        out_specs=vmem,
        scratch_shapes=[
            pltpu.VMEM((width, hidden), BF16),
            pltpu.VMEM((width, hidden), BF16),
            pltpu.VMEM((hidden, width), BF16),
            pltpu.VMEM((micro, PARTS, tok, part), BF16),
            pltpu.VMEM((micro, PARTS, tok, part), BF16),
            pltpu.VMEM((micro, PARTS, tok, part), BF16),
            pltpu.VMEM((micro, PARTS, tok, part), BF16),
            pltpu.VMEM((units, chips, blk, part), BF16),
            pltpu.VMEM((units, chips, blk, part), BF16),
            pltpu.VMEM((units, chips, blk, part), BF16),
            pltpu.VMEM((units, chips, blk, part), BF16),
            pltpu.VMEM((micro, chips * blk, top * PARTS * tok), BF16),
            pltpu.VMEM((micro, top * PARTS * tok, chips * blk), BF16),
            pltpu.VMEM((top * PARTS * tok, part), BF16),
            pltpu.VMEM((groups, PARTS * grp, part), BF16),
            pltpu.VMEM((chips * cap, width), BF16),
            pltpu.VMEM((micro, hidden // 256, chips * cap, 256), F32),
            pltpu.VMEM((micro, hidden // 256, chips * cap, 256), F32),
            pltpu.VMEM((chips * cap, hidden), BF16),
            pltpu.VMEM((chips * cap, hidden), BF16),
            dma((3,)),
            dma((3,)),
            dma((3,)),
            dma((units,)),
            dma((units, groups)),
            dma((units,)),
            dma((units, groups)),
            dma((units,)),
            dma((units,)),
        ],
        compiler_params=pltpu.CompilerParams(
            collective_id=0, has_side_effects=True, vmem_limit_bytes=60 * 1024 * 1024
        ),
        name="relay",
    )(
        tokens,
        norm_gain,
        target[:, None, :],
        target[:, :, None],
        gates,
        perm,
        perm_t,
        w_gate[0],
        w_up[0],
        w_down[0],
    )
    return result[None]


def solution(mesh):
    in_specs = (
        P(None, "expert", None),
        P("section", None),
        P("section", None, "expert"),
        P("section", None, "expert"),
        P("section", "expert", None),
        P("section", None, "expert", None),
        P("section", None, "expert", None),
    )
    out_specs = P("section", None, "expert", None)
    return jax.shard_map(body, mesh=mesh, in_specs=in_specs, out_specs=out_specs, check_vma=False)
```

time: 1840 us -> 603 us (0.33)
  waiting for transfers between devices: 1320 us -> 0 us
  Pallas kernels: 0 us -> 594 us
  local copies, waits for them, and re-layouts: 193 us -> 5.78 us
  starting transfers between devices: 156 us -> 0 us
  other arithmetic: 115 us -> 2.77 us
  matrix products: 40.4 us -> 0 us
    all_to_all x20 -> x0, waiting for transfers between devices: 1220 us -> none  [the longest x5 311 us: layer_forward(): lax.all_to_all(outgoing, 'expert', split_axis=0, concat_axis=0, tiled=True)]
    pallas_call x0 -> x1, Pallas kernels: none -> 594 us  [body(): pl.pallas_call(functools.partial(kernel, dims), out_shape=jax.ShapeDtypeS...]
    all_to_all x20 -> x0, starting transfers between devices: 128 us -> none  [the longest x5 38 us: layer_forward(): lax.all_to_all(outgoing, 'expert', split_axis=0, concat_axis=0, tiled=True)]
    ppermute x8 -> x0, waiting for transfers between devices: 103 us -> none  [shifted(): return lax.ppermute(x, axis, pairs)]
    cond x22 -> x0, local copies, waits for them, and re-layouts: 41.4 us -> none  [the longest x5 20.7 us: layer_forward(): lax.cond(active, expert_compute, expert_skipped, lax.all_to_all(outgoing,...]
    dot_general x12 -> x0, matrix products: 40.4 us -> none  [the longest x2 7.96 us: expert_compute(): jnp.einsum('ncd,dh->nch', payload, gate_mat, preferred_element_type=jnp.f...]
    reduce_sum x30 -> x1, other arithmetic: 35.3 us -> 0.18 us  [body(): position = jnp.sum(before * onehot, axis=-1)]
    reshape x25 -> x1, local copies, waits for them, and re-layouts: 36.3 us -> 1.27 us  [body(): jnp.broadcast_to(gates[:, :, None, :], (micro, top, PARTS, tok))]
  transfers between devices with their start and end apart: 28 -> 0, of which waited for: 28 -> 0; matrix products, arithmetic and copies ran while one was open for 1% -> 0% of each run, Pallas kernels for 0% -> 0%
where the time goes in v1:
time: 603 us
  Pallas kernels  594 us (99%)
    pallas_call x1, Pallas kernels, body(): pl.pallas_call(functools.partial(kernel, dims), out_shape=jax.ShapeDtypeS...  594 us

profile of v1, /device:TPU:1, one launch (start us, length us, event | category | flops | bytes accessed | tf_op | source)
XLA Modules:
  0.0 602.7 jit_solution(10864476012773893706)
XLA Ops:
  0.0 0.1 add.124
  0.1 0.1 add.125
  0.2 0.7 broadcast_in_dim.4
  0.9 0.8 copy.13
  1.6 0.1 eq.44
  1.8 0.1 fusion.2
  1.9 0.2 reduce_window_sum.11
  2.1 0.2 select_reduce_fusion
  2.3 0.1 reduce_sum.12
  2.4 0.1 copy.15
  2.5 0.1 add.123
  2.6 0.6 broadcast_add_fusion.1.route_row_ref
  3.2 0.7 fusion.1
  4.0 0.5 add.135
  4.4 0.9 broadcast_add_fusion.route_col_ref
  5.4 1.3 reshape.156.gate_col_ref
  6.6 594.1 %relay.1 = bf16[2,64,2560]{2,1,0:T(8,128)(2,1)} custom-call(bf16[2,64,2560]{2,1,0:T(8,128)(2,1)} %tokens_ref.1, f32[1,2560]{1,0:T(1,128)} %gain_ref.1, s32[2,1,512]{2,1,0:T(1,128)} %broadcast_add_fusion.1.route_row_ref, s32[2,512,1]{2,1,0:T(8,128)} %broadcast_add_fusion.route_col_ref, f32[2,512,1]{2,1,0:T(8,128)} %reshape.156.gate_col_ref, ...), custom_call_target="tpu_custom_call" | custom-call | tf_op jit(solution)/shard_map/relay/pallas_call | solution.py:394
  600.8 2.0 copy.20
  (4 shorter events, 0.0 us)

commit v2 on v1

--- a/solution.py
+++ b/solution.py
@@ -64,6 +64,7 @@
     b_recv,
     x_send,
     x_recv,
+    turn,
 ):
     sections, chips, cap, tok, width, micro, groups, half = dims
     blk = PARTS * cap
@@ -80,6 +81,8 @@
     mate = 2 * chip + (1 - core)
     my_group = lax.div(chip, per)
 
+    leads = (s == 0) & (core == 0)
+
     def other(j):
         return lax.rem(chip + j, chips)
 
@@ -158,6 +161,10 @@
         lax.fori_loop(1, chips, one, 0)
         pltpu.make_async_copy(src.at[u, chip], dst.at[u, chip], recv_sem.at[u, my_group]).start()
 
+    def sent_wait(u, buf, sem):
+        view = buf.at[u, pl.ds(0, chips - 1)]
+        pltpu.make_async_copy(view, view, sem.at[u]).wait()
+
     def group_wait(u, g, dst, recv_sem):
         view = dst.at[u, pl.ds(g * per, per)]
         pltpu.make_async_copy(view, view, recv_sem.at[u, g]).wait()
@@ -233,7 +240,17 @@
         sel = spread[m, :, :n] + spread[m, :, n:]
         out = mm(sel, stage[:n, :])
         send_a[u] = out.reshape(chips, blk, part).astype(BF16)
+
+        @pl.when((s == 0) & (core == 1) & (m == 0))
+        def _():
+            pl.semaphore_wait(turn, 1)
+
         scatter(u, send_a, recv_a, a_send, a_recv)
+
+        @pl.when(leads & (m == 0))
+        def _():
+            sent_wait(u, send_a, a_send)
+            pl.semaphore_signal(turn, inc=1, device_id={"expert": mate}, device_id_type=MESH)
 
         @pl.when(m == 0)
         def _():
@@ -340,9 +357,11 @@
         copy.wait_send()
 
     def drain(u, carry):
-        for buf, sem in ((send_a, a_send), (send_b, b_send)):
-            view = buf.at[u, pl.ds(0, chips - 1)]
-            pltpu.make_async_copy(view, view, sem.at[u]).wait()
+        @pl.when(jnp.logical_not(leads & (u == 0)))
+        def _():
+            sent_wait(u, send_a, a_send)
+
+        sent_wait(u, send_b, b_send)
         return carry
 
     lax.fori_loop(0, 2 * micro, drain, 0)
@@ -426,6 +445,7 @@
             dma((units, groups)),
             dma((units,)),
             dma((units,)),
+            pltpu.SemaphoreType.REGULAR,
         ],
         compiler_params=pltpu.CompilerParams(
             collective_id=0, has_side_effects=True, vmem_limit_bytes=60 * 1024 * 1024

time: 603 us -> 570 us (0.945)
  Pallas kernels: 594 us -> 559 us
    pallas_call x1, Pallas kernels: 594 us -> 559 us  [body(): pl.pallas_call(functools.partial(kernel, dims), out_shape=jax.ShapeDtypeS...]
where the time goes in v2:
time: 570 us; the launch traced here: 567 us
  Pallas kernels  559 us (98%)
  local copies, waits for them, and re-layouts  5.78 us (1%)
    pallas_call x1, Pallas kernels, body(): pl.pallas_call(functools.partial(kernel, dims), out_shape=jax.ShapeDtypeS...  559 us

profile of v2, /device:TPU:1, one launch (start us, length us, event | category | flops | bytes accessed | tf_op | source)
XLA Modules:
  0.0 567.1 jit_solution(12748782884113422091)
XLA Ops:
  0.0 0.1 add.124
  0.1 0.1 add.125
  0.2 0.7 broadcast_in_dim.4
  0.9 0.8 copy.13
  1.6 0.1 eq.44
  1.8 0.1 fusion.2
  1.9 0.2 reduce_window_sum.11
  2.1 0.2 select_reduce_fusion
  2.3 0.1 reduce_sum.12
  2.4 0.1 copy.15
  2.5 0.1 add.123
  2.6 0.6 broadcast_add_fusion.1.route_row_ref
  3.2 0.7 fusion.1
  4.0 0.5 add.135
  4.4 0.9 broadcast_add_fusion.route_col_ref
  5.4 1.3 reshape.156.gate_col_ref
  6.6 558.5 %relay.1 = bf16[2,64,2560]{2,1,0:T(8,128)(2,1)} custom-call(bf16[2,64,2560]{2,1,0:T(8,128)(2,1)} %tokens_ref.1, f32[1,2560]{1,0:T(1,128)} %gain_ref.1, s32[2,1,512]{2,1,0:T(1,128)} %broadcast_add_fusion.1.route_row_ref, s32[2,512,1]{2,1,0:T(8,128)} %broadcast_add_fusion.route_col_ref, f32[2,512,1]{2,1,0:T(8,128)} %reshape.156.gate_col_ref, ...), custom_call_target="tpu_custom_call" | custom-call | tf_op jit(solution)/shard_map/relay/pallas_call | solution.py:413
  565.2 2.0 copy.20
  (4 shorter events, 0.0 us)

commit v3 on v1

--- a/solution.py
+++ b/solution.py
@@ -64,6 +64,7 @@
     b_recv,
     x_send,
     x_recv,
+    turn,
 ):
     sections, chips, cap, tok, width, micro, groups, half = dims
     blk = PARTS * cap
@@ -73,6 +74,7 @@
     all_rows = chips * cap
     hidden = 2 * half
     step = 256
+    mark = 2
     s = lax.axis_index("section")
     ex = lax.axis_index("expert")
     core = lax.rem(ex, 2)
@@ -81,7 +83,8 @@
     my_group = lax.div(chip, per)
 
     def other(j):
-        return lax.rem(chip + j, chips)
+        g = lax.rem(my_group + lax.div(j, per), groups)
+        return g * per + lax.rem(chip + j, per)
 
     barrier = pltpu.get_barrier_semaphore()
 
@@ -151,6 +154,10 @@
         )
 
     def scatter(u, src, dst, send_sem, recv_sem):
+        @pl.when(core == 1)
+        def _():
+            pl.semaphore_wait(turn, 1)
+
         def one(j, carry):
             send_block(u, other(j), src, dst, send_sem, recv_sem).start()
             return carry
@@ -158,14 +165,24 @@
         lax.fori_loop(1, chips, one, 0)
         pltpu.make_async_copy(src.at[u, chip], dst.at[u, chip], recv_sem.at[u, my_group]).start()
 
-    def group_wait(u, g, dst, recv_sem):
+    def sent_wait(u, buf, sem):
+        view = buf.at[u, pl.ds(0, chips - 1)]
+        pltpu.make_async_copy(view, view, sem.at[u]).wait()
+
+    def group_wait(u, i, dst, recv_sem):
+        g = lax.rem(my_group + groups - i, groups)
         view = dst.at[u, pl.ds(g * per, per)]
         pltpu.make_async_copy(view, view, recv_sem.at[u, g]).wait()
 
+        @pl.when((core == 0) & (i == mark))
+        def _():
+            pl.semaphore_signal(turn, inc=1, device_id={"expert": mate}, device_id_type=MESH)
+
+        return g
+
     def arrive(u):
         def one(i, carry):
-            g = lax.rem(my_group + i, groups)
-            group_wait(u, g, recv_a, a_recv)
+            g = group_wait(u, i, recv_a, a_recv)
             got = recv_a[u, pl.ds(g * per, per)].astype(F32).reshape(per * blk, part).astype(BF16)
             sorted_rows = mm(perm_ref[...], got).astype(BF16)
             for q in range(PARTS):
@@ -186,8 +203,8 @@
         scatter(u, send_b, recv_b, b_send, b_recv)
 
     def wait_back(u):
-        def one(g, carry):
-            group_wait(u, g, recv_b, b_recv)
+        def one(i, carry):
+            group_wait(u, i, recv_b, b_recv)
             return carry
 
         lax.fori_loop(0, groups, one, 0)
@@ -233,6 +250,7 @@
         sel = spread[m, :, :n] + spread[m, :, n:]
         out = mm(sel, stage[:n, :])
         send_a[u] = out.reshape(chips, blk, part).astype(BF16)
+
         scatter(u, send_a, recv_a, a_send, a_recv)
 
         @pl.when(m == 0)
@@ -340,9 +358,8 @@
         copy.wait_send()
 
     def drain(u, carry):
-        for buf, sem in ((send_a, a_send), (send_b, b_send)):
-            view = buf.at[u, pl.ds(0, chips - 1)]
-            pltpu.make_async_copy(view, view, sem.at[u]).wait()
+        sent_wait(u, send_a, a_send)
+        sent_wait(u, send_b, b_send)
         return carry
 
     lax.fori_loop(0, 2 * micro, drain, 0)
@@ -426,6 +443,7 @@
             dma((units, groups)),
             dma((units,)),
             dma((units,)),
+            pltpu.SemaphoreType.REGULAR,
         ],
         compiler_params=pltpu.CompilerParams(
             collective_id=0, has_side_effects=True, vmem_limit_bytes=60 * 1024 * 1024

time: 603 us -> 550 us (0.912)
  Pallas kernels: 594 us -> 541 us
    pallas_call x1, Pallas kernels: 594 us -> 541 us  [body(): pl.pallas_call(functools.partial(kernel, dims), out_shape=jax.ShapeDtypeS...]
where the time goes in v3:
time: 550 us
  Pallas kernels  541 us (98%)
  local copies, waits for them, and re-layouts  5.78 us (1%)
    pallas_call x1, Pallas kernels, body(): pl.pallas_call(functools.partial(kernel, dims), out_shape=jax.ShapeDtypeS...  541 us

profile of v3, /device:TPU:1, one launch (start us, length us, event | category | flops | bytes accessed | tf_op | source)
XLA Modules:
  0.0 549.6 jit_solution(8323822692715963019)
XLA Ops:
  0.0 0.1 add.124
  0.1 0.1 add.125
  0.2 0.7 broadcast_in_dim.4
  0.9 0.8 copy.13
  1.6 0.1 eq.44
  1.8 0.1 fusion.2
  1.9 0.2 reduce_window_sum.11
  2.1 0.2 select_reduce_fusion
  2.3 0.1 reduce_sum.12
  2.4 0.1 copy.15
  2.5 0.1 add.123
  2.6 0.6 broadcast_add_fusion.1.route_row_ref
  3.2 0.7 fusion.1
  4.0 0.5 add.135
  4.4 0.9 broadcast_add_fusion.route_col_ref
  5.4 1.3 reshape.156.gate_col_ref
  6.6 541.0 %relay.1 = bf16[2,64,2560]{2,1,0:T(8,128)(2,1)} custom-call(bf16[2,64,2560]{2,1,0:T(8,128)(2,1)} %tokens_ref.1, f32[1,2560]{1,0:T(1,128)} %gain_ref.1, s32[2,1,512]{2,1,0:T(1,128)} %broadcast_add_fusion.1.route_row_ref, s32[2,512,1]{2,1,0:T(8,128)} %broadcast_add_fusion.route_col_ref, f32[2,512,1]{2,1,0:T(8,128)} %reshape.156.gate_col_ref, ...), custom_call_target="tpu_custom_call" | custom-call | tf_op jit(solution)/shard_map/relay/pallas_call | solution.py:411
  547.6 2.0 copy.20
  (4 shorter events, 0.0 us)

commit v4 on v3

v4 whole, which is shorter than its diff:
```python
import functools

import jax
import jax.numpy as jnp
from jax import lax
from jax.experimental import pallas as pl
from jax.experimental.pallas import tpu as pltpu
from jax.sharding import PartitionSpec as P

EPS = 1e-06
PARTS = 4
MESH = pl.DeviceIdType.MESH
F32 = jnp.float32
BF16 = jnp.bfloat16


def mm(a, b):
    return jnp.dot(a, b, preferred_element_type=F32)


def mm_nt(a, b):
    return lax.dot_general(a, b, (((1,), (1,)), ((), ())), preferred_element_type=F32)


def kernel(
    dims,
    tokens_ref,
    info_ref,
    perm_ref,
    perm_t_ref,
    w_gate_ref,
    w_up_ref,
    w_down_ref,
    out_ref,
    wg,
    wu,
    wd,
    info_near,
    cols,
    h_in,
    h_prev,
    h_next,
    g_in,
    g_next,
    o_in,
    send_a,
    recv_a,
    send_b,
    recv_b,
    spread,
    collect,
    stage,
    pieces,
    rows,
    pre_g,
    pre_u,
    act_a,
    act_b,
    w_local,
    w_send,
    w_recv,
    i_send,
    i_recv,
    a_send,
    a_recv,
    b_send,
    b_recv,
    x_send,
    x_recv,
    turn,
):
    sections, chips, cap, tok, width, micro, groups, half = dims
    blk = PARTS * cap
    part = width // PARTS
    per = chips // groups
    grp_rows = per * cap
    hidden = 2 * half
    n = PARTS * tok
    step = 256
    mark = 1
    last = sections - 1
    prev, own, after = 0, 1, 2
    s = lax.axis_index("section")
    ex = lax.axis_index("expert")
    core = lax.rem(ex, 2)
    chip = lax.div(ex, 2)
    mate = 2 * chip + (1 - core)
    my_group = lax.div(chip, per)

    def other(j):
        g = lax.rem(my_group + lax.div(j, per), groups)
        return g * per + lax.rem(chip + j, per)

    barrier = pltpu.get_barrier_semaphore()

    def greet(section, j):
        pl.semaphore_signal(
            barrier,
            inc=1,
            device_id={"section": section, "expert": 2 * other(j) + core},
            device_id_type=MESH,
        )

    def greet_own(j, carry):
        greet(s, j)
        return carry

    lax.fori_loop(1, chips, greet_own, 0)
    pl.semaphore_signal(barrier, inc=1, device_id={"expert": mate}, device_id_type=MESH)

    @pl.when(s > 0)
    def _():
        def one(j, carry):
            greet(s - 1, j)
            return carry

        lax.fori_loop(0, chips, one, 0)

    @pl.when(s < last)
    def _():
        def one(j, carry):
            greet(s + 1, j)
            return carry

        lax.fori_loop(0, chips, one, 0)

    local = [
        pltpu.make_async_copy(w_gate_ref, wg.at[:, :half], w_local.at[0]),
        pltpu.make_async_copy(w_up_ref, wu.at[:, :half], w_local.at[1]),
        pltpu.make_async_copy(w_down_ref, wd.at[:half, :], w_local.at[2]),
    ]
    for copy in local:
        copy.start()

    def columns(which, ref):
        cols[which] = jnp.transpose(ref[:, : 2 * n])

    def build(which, m):
        for k in range(2):
            at = k * n
            sub = cols[which, at : at + n, :][:, m : m + 1]
            ids = lax.broadcasted_iota(jnp.int32, (n, chips * blk), 1)
            collect[which, m, at : at + n, :] = jnp.where(
                ids == sub.astype(jnp.int32), 1.0, 0.0
            ).astype(BF16)

    for m in range(micro):
        for k in range(2):
            at = k * n
            lane = info_ref[m : m + 1, at : at + n].astype(jnp.int32)
            ids = lax.broadcasted_iota(jnp.int32, (chips * blk, n), 0)
            spread[m, :, at : at + n] = jnp.where(ids == lane, 1.0, 0.0).astype(BF16)

    ahead = lax.convert_element_type(s > 0, jnp.int32)
    behind = lax.convert_element_type(s < last, jnp.int32)
    pl.semaphore_wait(barrier, chips + chips * ahead + chips * behind)

    remote = [
        pltpu.make_async_remote_copy(
            src, dst, w_send.at[i], w_recv.at[i], device_id={"expert": mate}, device_id_type=MESH
        )
        for i, (src, dst) in enumerate(
            (
                (w_gate_ref, wg.at[:, half:]),
                (w_up_ref, wu.at[:, half:]),
                (w_down_ref, wd.at[half:, :]),
            )
        )
    ]
    for copy in remote:
        copy.start()

    def tell(slot, to):
        return pltpu.make_async_remote_copy(
            info_ref,
            info_near.at[slot],
            i_send.at[slot],
            i_recv.at[slot],
            device_id={"section": to},
            device_id_type=MESH,
        )

    @pl.when(s < last)
    def _():
        tell(0, s + 1).start()

    @pl.when(s > 0)
    def _():
        tell(1, s - 1).start()

    def hop(src, dst, m, kind, to):
        return pltpu.make_async_remote_copy(
            src.at[m],
            dst.at[m],
            x_send.at[kind, m],
            x_recv.at[kind, m],
            device_id={"section": to},
            device_id_type=MESH,
        )

    h_on = functools.partial(hop, h_in, h_prev, kind=0)
    h_back = functools.partial(hop, h_in, h_next, kind=1)
    g_back = functools.partial(hop, g_in, g_next, kind=2)
    o_on = functools.partial(hop, g_in, o_in, kind=3)

    def send_wait(buf, u, sem, count):
        view = buf.at[u, pl.ds(0, count)]
        pltpu.make_async_copy(view, view, sem.at[u]).wait()

    def group_wait(buf, u, i, sem):
        g = lax.rem(my_group + groups - i, groups)
        view = buf.at[u, pl.ds(g * per, per)]
        pltpu.make_async_copy(view, view, sem.at[u, g]).wait()
        return g

    def dispatch(u, m):
        send_a[u] = mm(
            spread[m] if stage_full[0] else spread[m, :, :n] + spread[m, :, n:],
            stage[...] if stage_full[0] else stage[:n, :],
        ).reshape(chips, blk, part).astype(BF16)

        @pl.when(core == 1)
        def _():
            pl.semaphore_wait(turn, 1)

        def one(j, carry):
            d = other(j)
            pltpu.make_async_remote_copy(
                send_a.at[u, d],
                recv_a.at[u, chip],
                a_send.at[u],
                a_recv.at[u, my_group],
                device_id={"expert": 2 * d + core},
                device_id_type=MESH,
            ).start()
            return carry

        lax.fori_loop(1, chips, one, 0)
        pltpu.make_async_copy(send_a.at[u, chip], recv_a.at[u, chip], a_recv.at[u, my_group]).start()

    def arrive(u):
        def one(i, carry):
            g = group_wait(recv_a, u, i, a_recv)

            @pl.when((core == 0) & (i == mark))
            def _():
                pl.semaphore_signal(turn, inc=1, device_id={"expert": mate}, device_id_type=MESH)

            got = recv_a[u, pl.ds(g * per, per)].astype(F32).reshape(per * blk, part).astype(BF16)
            sorted_rows = mm(perm_ref[...], got).astype(BF16)
            for q in range(PARTS):
                rows[pl.ds(g * grp_rows, grp_rows), q * part : (q + 1) * part] = sorted_rows[
                    q * grp_rows : (q + 1) * grp_rows
                ]
            return carry

        lax.fori_loop(0, groups, one, 0)

    def give_back(u, to, slot):
        def one(i, carry):
            g = lax.rem(my_group + i, groups)
            got = mm(perm_t_ref[...], pieces[g])
            send_b[u, pl.ds(g * per, per)] = got.reshape(per, blk, part).astype(BF16)

            def block(j, inner):
                d = g * per + lax.rem(chip + j, per)

                @pl.when(jnp.logical_or(d != chip, to != s))
                def _():
                    pltpu.make_async_remote_copy(
                        send_b.at[u, d],
                        recv_b.at[slot, chip],
                        b_send.at[u],
                        b_recv.at[slot, my_group],
                        device_id={"section": to, "expert": 2 * d + core},
                        device_id_type=MESH,
                    ).start()

                return inner

            return lax.fori_loop(0, per, block, carry)

        lax.fori_loop(0, groups, one, 0)

        @pl.when(to == s)
        def _():
            pltpu.make_async_copy(
                send_b.at[u, chip], recv_b.at[slot, chip], b_recv.at[slot, my_group]
            ).start()

    def wait_back(slot):
        def one(i, carry):
            group_wait(recv_b, slot, i, b_recv)
            return carry

        lax.fori_loop(0, groups, one, 0)
        return recv_b[slot].astype(F32).reshape(chips * blk, part).astype(BF16)

    def put_pieces(q, value):
        for g in range(groups):
            pieces[g, pl.ds(q * grp_rows, grp_rows), :] = value[g * grp_rows : (g + 1) * grp_rows]

    def gate_column(which, m):
        return jnp.where(m == 0, cols[which][:, micro : micro + 1], cols[which][:, micro + 1 : micro + 2])

    def inverse_rms(h):
        total = jnp.sum(jnp.sum(h * h, axis=-1, keepdims=True), axis=0)
        return lax.rsqrt(total / width + EPS)

    def mix(h, slot, which, m):
        picked = mm(collect[which, m], wait_back(slot)) * gate_column(which, m)
        mixture = picked[:n] + picked[n:]
        return (h.astype(F32) + mixture.reshape(PARTS, tok, part)).astype(BF16)

    def grad(g, h, gain, slot, which, m):
        sel = collect[which, m, :n] + collect[which, m, n:]
        total = mm(sel, wait_back(slot)).reshape(PARTS, tok, part)
        h = h.astype(F32)
        inv = inverse_rms(h)
        weighted = total * jnp.stack([gain[2 * micro + q : 2 * micro + q + 1, :] for q in range(PARTS)])
        dot = jnp.sum(jnp.sum(h * weighted, axis=-1, keepdims=True), axis=0) / width
        change = inv[None] * weighted - h * (inv * inv * inv * dot)[None]
        return (g.astype(F32) + change).astype(BF16)

    columns(own, info_ref)
    stage_full = [False]

    @pl.when(s > 0)
    def _():
        tell(0, s).wait_recv()
        columns(prev, info_near.at[0])
        for m in range(micro):
            build(prev, m)

    def forward(m, carry):
        u = m

        @pl.when(s == 0)
        def _():
            for q in range(PARTS):
                h_in[m, q] = tokens_ref[m, :, q * part : (q + 1) * part]

        @pl.when(s > 0)
        def _():
            h_on(m=m, to=s).wait_recv()
            h_in[m] = mix(h_prev[m], m, prev, m)

        inv = inverse_rms(h_in[m].astype(F32))
        for q in range(PARTS):
            gain = info_ref[2 * micro + q : 2 * micro + q + 1, :]
            stage[pl.ds(q * tok, tok), :] = (h_in[m, q].astype(F32) * inv * gain).astype(BF16)
        dispatch(u, m)

        @pl.when(s < last)
        def _():
            h_on(m=m, to=s + 1).start()

        @pl.when(s > 0)
        def _():
            h_back(m=m, to=s - 1).start()

        @pl.when(m == 0)
        def _():
            for copy in local:
                copy.wait()
            for copy in remote:
                copy.wait_recv()
            for i in range(micro):
                build(own, i)

            @pl.when(s < last)
            def _():
                tell(1, s).wait_recv()
                columns(after, info_near.at[1])
                for i in range(micro):
                    build(after, i)

        arrive(u)

        def first(i, carry):
            at = pl.ds(pl.multiple_of(i * step, step), step)
            gate = mm(rows[...], wg[:, at])
            up = mm(rows[...], wu[:, at])
            pre_g[m, i] = gate
            pre_u[m, i] = up
            act_a[:, at] = (gate * jax.nn.sigmoid(gate) * up).astype(BF16)
            return carry

        lax.fori_loop(0, hidden // step, first, 0)

        def second(q, carry):
            at = pl.ds(pl.multiple_of(q * part, part), part)
            put_pieces(q, mm(act_a[...], wd[:, at]).astype(BF16))
            return carry

        lax.fori_loop(0, PARTS, second, 0)
        give_back(u, jnp.minimum(s + 1, last), m + micro * (1 - behind))

        @pl.when(s == last)
        def _():
            g_in[m] = mix(h_in[m], micro + m, own, m)

        return carry

    lax.fori_loop(0, micro, forward, 0)
    stage_full[0] = True

    def backward(m, carry):
        u = micro + m

        @pl.when(s < last)
        def _():
            g_back(m=m, to=s).wait_recv()
            h_back(m=m, to=s).wait_recv()
            g_in[m] = grad(g_next[m], h_next[m], info_near.at[1], 2 * micro + m, after, m)

        upstream = g_in[m].astype(F32).reshape(n, part)
        gates = gate_column(own, m)
        stage[:n, :] = (gates[:n] * upstream).astype(BF16)
        stage[n:, :] = (gates[n:] * upstream).astype(BF16)
        dispatch(u, m)

        @pl.when(s > 0)
        def _():
            g_back(m=m, to=s - 1).start()

        @pl.when(s < last)
        def _():
            o_on(m=m, to=s + 1).start()

        arrive(u)

        def first(i, carry):
            at = pl.ds(pl.multiple_of(i * step, step), step)
            grad_hidden = mm_nt(rows[...], wd[at, :])
            gate = pre_g[m, i]
            up = pre_u[m, i]
            logistic = jax.nn.sigmoid(gate)
            act_a[:, at] = (grad_hidden * up * logistic * (1.0 + gate * (1.0 - logistic))).astype(BF16)
            act_b[:, at] = (grad_hidden * gate * logistic).astype(BF16)
            return carry

        lax.fori_loop(0, hidden // step, first, 0)

        def second(q, carry):
            at = pl.ds(pl.multiple_of(q * part, part), part)
            value = mm_nt(act_a[...], wg[at, :]) + mm_nt(act_b[...], wu[at, :])
            put_pieces(q, value.astype(BF16))
            return carry

        lax.fori_loop(0, PARTS, second, 0)
        give_back(u, jnp.maximum(s - 1, 0), 2 * micro + m + micro * (1 - ahead))

        @pl.when(s == 0)
        def _():
            value = grad(g_in[m], h_in[m], info_ref, 3 * micro + m, own, m)
            for q in range(PARTS):
                out_ref[m, :, q * part : (q + 1) * part] = value[q]

        return carry

    lax.fori_loop(0, micro, backward, 0)

    @pl.when(s > 0)
    def _():
        for m in range(micro):
            o_on(m=m, to=s).wait_recv()
            for q in range(PARTS):
                out_ref[m, :, q * part : (q + 1) * part] = o_in[m, q]

    for copy in remote:
        copy.wait_send()

    @pl.when(s < last)
    def _():
        tell(0, s).wait_send()

    @pl.when(s > 0)
    def _():
        tell(1, s).wait_send()

    def drain(u, carry):
        send_wait(send_a, u, a_send, chips - 1)
        stays = jnp.where(u < micro, s == last, s == 0)

        @pl.when(stays)
        def _():
            send_wait(send_b, u, b_send, chips - 1)

        @pl.when(jnp.logical_not(stays))
        def _():
            send_wait(send_b, u, b_send, chips)

        return carry

    lax.fori_loop(0, 2 * micro, drain, 0)
    for m in range(micro):

        @pl.when(s < last)
        def _():
            h_on(m=m, to=s).wait_send()
            o_on(m=m, to=s).wait_send()

        @pl.when(s > 0)
        def _():
            h_back(m=m, to=s).wait_send()
            g_back(m=m, to=s).wait_send()


def body(tokens, norm_gain, w_gate, w_up, w_down, route_ids, route_gates):
    sections = lax.axis_size("section")
    chips = lax.axis_size("expert") // 2
    micro, tok, width = tokens.shape
    top = route_ids.shape[-1]
    half = w_gate.shape[-1]
    hidden = 2 * half
    cap = max(2, (4 * tok * top + 3 * chips - 1) // (3 * chips))
    blk = PARTS * cap
    part = width // PARTS
    groups = 4
    per = chips // groups
    grp = per * cap
    units = 2 * micro

    flat = route_ids[0].reshape(micro, tok * top)
    onehot = (flat[:, :, None] == jnp.arange(chips, dtype=jnp.int32)).astype(jnp.int32)
    before = jnp.cumsum(onehot, axis=1) - onehot
    position = jnp.sum(before * onehot, axis=-1)
    first = (flat * blk + position).reshape(micro, tok, top).transpose(0, 2, 1)
    offset = jnp.arange(PARTS, dtype=jnp.int32) * cap
    target = (first[:, :, None, :] + offset[None, None, :, None]).reshape(micro, top * PARTS * tok)
    gates = route_gates[0].transpose(0, 2, 1)
    gates = jnp.broadcast_to(gates[:, :, None, :], (micro, top, PARTS, tok)).reshape(micro, -1)
    pad = ((0, 0), (0, part - top * PARTS * tok))
    info = jnp.concatenate(
        [
            jnp.pad(target.astype(F32), pad),
            jnp.pad(gates, pad),
            norm_gain.reshape(PARTS, part),
            jnp.zeros((16 - 2 * micro - PARTS, part), F32),
        ]
    )

    src = jnp.arange(per * blk, dtype=jnp.int32)
    dest = (src % blk // cap) * grp + src // blk * cap + src % cap
    perm_t = (dest[:, None] == src[None, :]).astype(BF16)
    perm = (src[:, None] == dest[None, :]).astype(BF16)

    dims = (sections, chips, cap, tok, width, micro, groups, half)
    vmem = pl.BlockSpec(memory_space=pltpu.VMEM)
    hbm = pl.BlockSpec(memory_space=pl.ANY)
    dma = pltpu.SemaphoreType.DMA
    result = pl.pallas_call(
        functools.partial(kernel, dims),
        out_shape=jax.ShapeDtypeStruct((micro, tok, width), BF16),
        in_specs=[vmem] * 4 + [hbm] * 3,
        out_specs=vmem,
        scratch_shapes=[
            pltpu.VMEM((width, hidden), BF16),
            pltpu.VMEM((width, hidden), BF16),
            pltpu.VMEM((hidden, width), BF16),
            pltpu.VMEM((2, 16, part), F32),
            pltpu.VMEM((3, top * PARTS * tok, 16), F32),
        ]
        + [pltpu.VMEM((micro, PARTS, tok, part), BF16)] * 6
        + [pltpu.VMEM((units, chips, blk, part), BF16)] * 3
        + [
            pltpu.VMEM((2 * units, chips, blk, part), BF16),
            pltpu.VMEM((micro, chips * blk, top * PARTS * tok), BF16),
            pltpu.VMEM((3, micro, top * PARTS * tok, chips * blk), BF16),
            pltpu.VMEM((top * PARTS * tok, part), BF16),
            pltpu.VMEM((groups, PARTS * grp, part), BF16),
            pltpu.VMEM((chips * cap, width), BF16),
            pltpu.VMEM((micro, hidden // 256, chips * cap, 256), F32),
            pltpu.VMEM((micro, hidden // 256, chips * cap, 256), F32),
            pltpu.VMEM((chips * cap, hidden), BF16),
            pltpu.VMEM((chips * cap, hidden), BF16),
            dma((3,)),
            dma((3,)),
            dma((3,)),
            dma((2,)),
            dma((2,)),
            dma((units,)),
            dma((units, groups)),
            dma((units,)),
            dma((2 * units, groups)),
            dma((4, micro)),
            dma((4, micro)),
            pltpu.SemaphoreType.REGULAR,
        ],
        compiler_params=pltpu.CompilerParams(
            collective_id=0, has_side_effects=True, vmem_limit_bytes=60 * 1024 * 1024
        ),
        name="relay",
    )(
        tokens,
        info,
        perm,
        perm_t,
        w_gate[0],
        w_up[0],
        w_down[0],
    )
    return result[None]


def solution(mesh):
    in_specs = (
        P(None, "expert", None),
        P("section", None),
        P("section", None, "expert"),
        P("section", None, "expert"),
        P("section", "expert", None),
        P("section", None, "expert", None),
        P("section", None, "expert", None),
    )
    out_specs = P("section", None, "expert", None)
    return jax.shard_map(body, mesh=mesh, in_specs=in_specs, out_specs=out_specs, check_vma=False)
```

time: 550 us -> 528 us (0.960)
  Pallas kernels: 541 us -> 521 us
    pallas_call x1, Pallas kernels: 541 us -> 521 us  [body(): pl.pallas_call(functools.partial(kernel, dims), out_shape=jax.ShapeDtypeS...]
where the time goes in v4:
time: 528 us
  Pallas kernels  521 us (99%)
    pallas_call x1, Pallas kernels, body(): pl.pallas_call(functools.partial(kernel, dims), out_shape=jax.ShapeDtypeS...  521 us

profile of v4, /device:TPU:1, one launch (start us, length us, event | category | flops | bytes accessed | tf_op | source)
XLA Modules:
  0.0 528.1 jit_solution(3206518562952120421)
XLA Ops:
  0.0 0.1 pad.12.clone
  0.1 0.1 add.105
  0.2 0.1 add.106
  0.3 0.7 broadcast_in_dim.6
  0.9 0.1 reshape.93
  1.0 0.7 reduce
  1.8 0.8 copy.8
  2.6 0.1 eq.44
  2.7 0.1 fusion.2
  2.8 0.2 reduce_window_sum.11
  3.0 0.2 select_reduce_fusion
  3.2 0.1 reduce_sum.12
  3.4 0.1 copy.10
  3.5 0.1 add.104
  3.6 0.7 fusion.5.info_ref
  4.2 0.7 fusion.1
  5.0 521.1 %relay.1 = bf16[2,64,2560]{2,1,0:T(8,128)(2,1)} custom-call(bf16[2,64,2560]{2,1,0:T(8,128)(2,1)} %tokens_ref.1, f32[16,640]{1,0:T(8,128)} %fusion.5.info_ref, bf16[192,192]{1,0:T(8,128)(2,1)} %get-tuple-element.6.perm_ref, bf16[192,192]{1,0:T(8,128)(2,1)} %get-tuple-element.5.perm_t_ref, bf16[2560,384]{1,0:T(8,128)(2,1)} %bitcast.16, ...), custom_call_target="tpu_custom_call" | custom-call | tf_op jit(solution)/shard_map/relay/pallas_call | solution.py:553
  526.1 2.0 copy.12
  (7 shorter events, 0.1 us)

commit v5 on v4

--- a/solution.py
+++ b/solution.py
@@ -9,6 +9,7 @@
 
 EPS = 1e-06
 PARTS = 4
+CHUNKS = 4
 MESH = pl.DeviceIdType.MESH
 F32 = jnp.float32
 BF16 = jnp.bfloat16
@@ -74,6 +75,7 @@
     part = width // PARTS
     per = chips // groups
     grp_rows = per * cap
+    run = groups // CHUNKS
     hidden = 2 * half
     n = PARTS * tok
     step = 256
@@ -238,8 +240,9 @@
         lax.fori_loop(1, chips, one, 0)
         pltpu.make_async_copy(send_a.at[u, chip], recv_a.at[u, chip], a_recv.at[u, my_group]).start()
 
-    def arrive(u):
-        def one(i, carry):
+    def arrive(u, c):
+        def one(t, carry):
+            i = c * run + t
             g = group_wait(recv_a, u, i, a_recv)
 
             @pl.when((core == 0) & (i == mark))
@@ -249,17 +252,17 @@
             got = recv_a[u, pl.ds(g * per, per)].astype(F32).reshape(per * blk, part).astype(BF16)
             sorted_rows = mm(perm_ref[...], got).astype(BF16)
             for q in range(PARTS):
-                rows[pl.ds(g * grp_rows, grp_rows), q * part : (q + 1) * part] = sorted_rows[
+                rows[pl.ds(t * grp_rows, grp_rows), q * part : (q + 1) * part] = sorted_rows[
                     q * grp_rows : (q + 1) * grp_rows
                 ]
             return carry
 
-        lax.fori_loop(0, groups, one, 0)
-
-    def give_back(u, to, slot):
-        def one(i, carry):
-            g = lax.rem(my_group + i, groups)
-            got = mm(perm_t_ref[...], pieces[g])
+        lax.fori_loop(0, run, one, 0)
+
+    def give_back(u, c, to, slot):
+        def one(t, carry):
+            g = lax.rem(my_group + groups - c * run - t, groups)
+            got = mm(perm_t_ref[...], pieces[t])
             send_b[u, pl.ds(g * per, per)] = got.reshape(per, blk, part).astype(BF16)
 
             def block(j, inner):
@@ -280,9 +283,9 @@
 
             return lax.fori_loop(0, per, block, carry)
 
-        lax.fori_loop(0, groups, one, 0)
-
-        @pl.when(to == s)
+        lax.fori_loop(0, run, one, 0)
+
+        @pl.when((to == s) & (c == 0))
         def _():
             pltpu.make_async_copy(
                 send_b.at[u, chip], recv_b.at[slot, chip], b_recv.at[slot, my_group]
@@ -297,8 +300,8 @@
         return recv_b[slot].astype(F32).reshape(chips * blk, part).astype(BF16)
 
     def put_pieces(q, value):
-        for g in range(groups):
-            pieces[g, pl.ds(q * grp_rows, grp_rows), :] = value[g * grp_rows : (g + 1) * grp_rows]
+        for t in range(run):
+            pieces[t, pl.ds(q * grp_rows, grp_rows), :] = value[t * grp_rows : (t + 1) * grp_rows]
 
     def gate_column(which, m):
         return jnp.where(m == 0, cols[which][:, micro : micro + 1], cols[which][:, micro + 1 : micro + 2])
@@ -375,26 +378,30 @@
                 for i in range(micro):
                     build(after, i)
 
-        arrive(u)
-
-        def first(i, carry):
-            at = pl.ds(pl.multiple_of(i * step, step), step)
-            gate = mm(rows[...], wg[:, at])
-            up = mm(rows[...], wu[:, at])
-            pre_g[m, i] = gate
-            pre_u[m, i] = up
-            act_a[:, at] = (gate * jax.nn.sigmoid(gate) * up).astype(BF16)
+        def chunk(c, carry):
+            arrive(u, c)
+
+            def first(i, carry):
+                at = pl.ds(pl.multiple_of(i * step, step), step)
+                gate = mm(rows[...], wg[:, at])
+                up = mm(rows[...], wu[:, at])
+                pre_g[m, c, i] = gate
+                pre_u[m, c, i] = up
+                act_a[:, at] = (gate * jax.nn.sigmoid(gate) * up).astype(BF16)
+                return carry
+
+            lax.fori_loop(0, hidden // step, first, 0)
+
+            def second(q, carry):
+                at = pl.ds(pl.multiple_of(q * part, part), part)
+                put_pieces(q, mm(act_a[...], wd[:, at]).astype(BF16))
+                return carry
+
+            lax.fori_loop(0, PARTS, second, 0)
+            give_back(u, c, jnp.minimum(s + 1, last), m + micro * (1 - behind))
             return carry
 
-        lax.fori_loop(0, hidden // step, first, 0)
-
-        def second(q, carry):
-            at = pl.ds(pl.multiple_of(q * part, part), part)
-            put_pieces(q, mm(act_a[...], wd[:, at]).astype(BF16))
-            return carry
-
-        lax.fori_loop(0, PARTS, second, 0)
-        give_back(u, jnp.minimum(s + 1, last), m + micro * (1 - behind))
+        lax.fori_loop(0, CHUNKS, chunk, 0)
 
         @pl.when(s == last)
         def _():
@@ -428,28 +435,33 @@
         def _():
             o_on(m=m, to=s + 1).start()
 
-        arrive(u)
-
-        def first(i, carry):
-            at = pl.ds(pl.multiple_of(i * step, step), step)
-            grad_hidden = mm_nt(rows[...], wd[at, :])
-            gate = pre_g[m, i]
-            up = pre_u[m, i]
-            logistic = jax.nn.sigmoid(gate)
-            act_a[:, at] = (grad_hidden * up * logistic * (1.0 + gate * (1.0 - logistic))).astype(BF16)
-            act_b[:, at] = (grad_hidden * gate * logistic).astype(BF16)
+        def chunk(c, carry):
+            arrive(u, c)
+
+            def first(i, carry):
+                at = pl.ds(pl.multiple_of(i * step, step), step)
+                grad_hidden = mm_nt(rows[...], wd[at, :])
+                gate = pre_g[m, c, i]
+                up = pre_u[m, c, i]
+                logistic = jax.nn.sigmoid(gate)
+                slope = logistic * (1.0 + gate * (1.0 - logistic))
+                act_a[:, at] = (grad_hidden * up * slope).astype(BF16)
+                act_b[:, at] = (grad_hidden * gate * logistic).astype(BF16)
+                return carry
+
+            lax.fori_loop(0, hidden // step, first, 0)
+
+            def second(q, carry):
+                at = pl.ds(pl.multiple_of(q * part, part), part)
+                value = mm_nt(act_a[...], wg[at, :]) + mm_nt(act_b[...], wu[at, :])
+                put_pieces(q, value.astype(BF16))
+                return carry
+
+            lax.fori_loop(0, PARTS, second, 0)
+            give_back(u, c, jnp.maximum(s - 1, 0), 2 * micro + m + micro * (1 - ahead))
             return carry
 
-        lax.fori_loop(0, hidden // step, first, 0)
-
-        def second(q, carry):
-            at = pl.ds(pl.multiple_of(q * part, part), part)
-            value = mm_nt(act_a[...], wg[at, :]) + mm_nt(act_b[...], wu[at, :])
-            put_pieces(q, value.astype(BF16))
-            return carry
-
-        lax.fori_loop(0, PARTS, second, 0)
-        give_back(u, jnp.maximum(s - 1, 0), 2 * micro + m + micro * (1 - ahead))
+        lax.fori_loop(0, CHUNKS, chunk, 0)
 
         @pl.when(s == 0)
         def _():
@@ -521,6 +533,7 @@
     per = chips // groups
     grp = per * cap
     units = 2 * micro
+    chunk_rows = chips * cap // CHUNKS
 
     flat = route_ids[0].reshape(micro, tok * top)
     onehot = (flat[:, :, None] == jnp.arange(chips, dtype=jnp.int32)).astype(jnp.int32)
@@ -569,12 +582,12 @@
             pltpu.VMEM((micro, chips * blk, top * PARTS * tok), BF16),
             pltpu.VMEM((3, micro, top * PARTS * tok, chips * blk), BF16),
             pltpu.VMEM((top * PARTS * tok, part), BF16),
-            pltpu.VMEM((groups, PARTS * grp, part), BF16),
-            pltpu.VMEM((chips * cap, width), BF16),
-            pltpu.VMEM((micro, hidden // 256, chips * cap, 256), F32),
-            pltpu.VMEM((micro, hidden // 256, chips * cap, 256), F32),
-            pltpu.VMEM((chips * cap, hidden), BF16),
-            pltpu.VMEM((chips * cap, hidden), BF16),
+            pltpu.VMEM((groups // CHUNKS, PARTS * grp, part), BF16),
+            pltpu.VMEM((chunk_rows, width), BF16),
+            pltpu.VMEM((micro, CHUNKS, hidden // 256, chunk_rows, 256), F32),
+            pltpu.VMEM((micro, CHUNKS, hidden // 256, chunk_rows, 256), F32),
+            pltpu.VMEM((chunk_rows, hidden), BF16),
+            pltpu.VMEM((chunk_rows, hidden), BF16),
             dma((3,)),
             dma((3,)),
             dma((3,)),

time: 528 us -> 456 us (0.86)
  Pallas kernels: 521 us -> 449 us
    pallas_call x1, Pallas kernels: 521 us -> 449 us  [body(): pl.pallas_call(functools.partial(kernel, dims), out_shape=jax.ShapeDtypeS...]
where the time goes in v5:
time: 456 us
  Pallas kernels  449 us (98%)
    pallas_call x1, Pallas kernels, body(): pl.pallas_call(functools.partial(kernel, dims), out_shape=jax.ShapeDtypeS...  449 us

profile of v5, /device:TPU:1, one launch (start us, length us, event | category | flops | bytes accessed | tf_op | source)
XLA Modules:
  0.0 455.9 jit_solution(1243193784668901155)
XLA Ops:
  0.0 0.1 pad.12.clone
  0.1 0.1 add.105
  0.2 0.1 add.106
  0.3 0.7 broadcast_in_dim.6
  0.9 0.1 reshape.93
  1.0 0.7 reduce
  1.8 0.8 copy.8
  2.6 0.1 eq.44
  2.7 0.1 fusion.2
  2.8 0.2 reduce_window_sum.11
  3.0 0.2 select_reduce_fusion
  3.2 0.1 reduce_sum.12
  3.4 0.1 copy.10
  3.5 0.1 add.104
  3.6 0.7 fusion.5.info_ref
  4.2 0.7 fusion.1
  5.0 449.0 %relay.1 = bf16[2,64,2560]{2,1,0:T(8,128)(2,1)} custom-call(bf16[2,64,2560]{2,1,0:T(8,128)(2,1)} %tokens_ref.1, f32[16,640]{1,0:T(8,128)} %fusion.5.info_ref, bf16[192,192]{1,0:T(8,128)(2,1)} %get-tuple-element.6.perm_ref, bf16[192,192]{1,0:T(8,128)(2,1)} %get-tuple-element.5.perm_t_ref, bf16[2560,384]{1,0:T(8,128)(2,1)} %bitcast.16, ...), custom_call_target="tpu_custom_call" | custom-call | tf_op jit(solution)/shard_map/relay/pallas_call | solution.py:566
  454.0 2.0 copy.12
  (7 shorter events, 0.1 us)

commit v6 on v5

--- a/solution.py
+++ b/solution.py
@@ -69,6 +69,7 @@
     x_send,
     x_recv,
     turn,
+    entered,
 ):
     sections, chips, cap, tok, width, micro, groups, half = dims
     blk = PARTS * cap
@@ -95,36 +96,24 @@
 
     barrier = pltpu.get_barrier_semaphore()
 
-    def greet(section, j):
+    def greet(j, carry):
         pl.semaphore_signal(
-            barrier,
-            inc=1,
-            device_id={"section": section, "expert": 2 * other(j) + core},
-            device_id_type=MESH,
+            barrier, inc=1, device_id={"expert": 2 * other(j) + core}, device_id_type=MESH
         )
-
-    def greet_own(j, carry):
-        greet(s, j)
         return carry
 
-    lax.fori_loop(1, chips, greet_own, 0)
+    turns = jnp.where(s == last, micro, 2 * micro)
+
+    lax.fori_loop(1, chips, greet, 0)
     pl.semaphore_signal(barrier, inc=1, device_id={"expert": mate}, device_id_type=MESH)
 
     @pl.when(s > 0)
     def _():
-        def one(j, carry):
-            greet(s - 1, j)
-            return carry
-
-        lax.fori_loop(0, chips, one, 0)
+        pl.semaphore_signal(barrier, inc=1, device_id={"section": s - 1}, device_id_type=MESH)
 
     @pl.when(s < last)
     def _():
-        def one(j, carry):
-            greet(s + 1, j)
-            return carry
-
-        lax.fori_loop(0, chips, one, 0)
+        pl.semaphore_signal(barrier, inc=1, device_id={"section": s + 1}, device_id_type=MESH)
 
     local = [
         pltpu.make_async_copy(w_gate_ref, wg.at[:, :half], w_local.at[0]),
@@ -146,16 +135,25 @@
                 ids == sub.astype(jnp.int32), 1.0, 0.0
             ).astype(BF16)
 
-    for m in range(micro):
+    def build_spread(m, ref=info_ref, place=0):
         for k in range(2):
             at = k * n
-            lane = info_ref[m : m + 1, at : at + n].astype(jnp.int32)
+            lane = ref[m : m + 1, at : at + n].astype(jnp.int32)
             ids = lax.broadcasted_iota(jnp.int32, (chips * blk, n), 0)
-            spread[m, :, at : at + n] = jnp.where(ids == lane, 1.0, 0.0).astype(BF16)
-
+            spread[place + m, :, at : at + n] = jnp.where(ids == lane, 1.0, 0.0).astype(BF16)
+
+    build_spread(0)
     ahead = lax.convert_element_type(s > 0, jnp.int32)
     behind = lax.convert_element_type(s < last, jnp.int32)
-    pl.semaphore_wait(barrier, chips + chips * ahead + chips * behind)
+    pl.semaphore_wait(barrier, chips + ahead + behind)
+
+    @pl.when(s > 0)
+    def _():
+        pl.semaphore_signal(entered.at[1], inc=1, device_id={"section": s - 1}, device_id_type=MESH)
+
+    @pl.when(s < last)
+    def _():
+        pl.semaphore_signal(entered.at[0], inc=1, device_id={"section": s + 1}, device_id_type=MESH)
 
     remote = [
         pltpu.make_async_remote_copy(
@@ -215,13 +213,11 @@
         pltpu.make_async_copy(view, view, sem.at[u, g]).wait()
         return g
 
-    def dispatch(u, m):
-        send_a[u] = mm(
-            spread[m] if stage_full[0] else spread[m, :, :n] + spread[m, :, n:],
-            stage[...] if stage_full[0] else stage[:n, :],
-        ).reshape(chips, blk, part).astype(BF16)
-
-        @pl.when(core == 1)
+    def fill(u, sel, value):
+        send_a[u] = mm(sel, value).reshape(chips, blk, part).astype(BF16)
+
+    def dispatch(u):
+        @pl.when(jnp.logical_or(core == 1, u > 0))
         def _():
             pl.semaphore_wait(turn, 1)
 
@@ -240,14 +236,25 @@
         lax.fori_loop(1, chips, one, 0)
         pltpu.make_async_copy(send_a.at[u, chip], recv_a.at[u, chip], a_recv.at[u, my_group]).start()
 
+    def dispatch_last(m):
+        def one(j, carry):
+            d = other(j)
+            pltpu.make_async_remote_copy(
+                send_a.at[2 * micro + m, d],
+                recv_a.at[micro + m, chip],
+                a_send.at[2 * micro + m],
+                a_recv.at[micro + m, my_group],
+                device_id={"section": last, "expert": 2 * d + core},
+                device_id_type=MESH,
+            ).start()
+            return carry
+
+        lax.fori_loop(0, chips, one, 0)
+
     def arrive(u, c):
         def one(t, carry):
             i = c * run + t
             g = group_wait(recv_a, u, i, a_recv)
-
-            @pl.when((core == 0) & (i == mark))
-            def _():
-                pl.semaphore_signal(turn, inc=1, device_id={"expert": mate}, device_id_type=MESH)
 
             got = recv_a[u, pl.ds(g * per, per)].astype(F32).reshape(per * blk, part).astype(BF16)
             sorted_rows = mm(perm_ref[...], got).astype(BF16)
@@ -285,6 +292,10 @@
 
         lax.fori_loop(0, run, one, 0)
 
+        @pl.when((u < turns - 1 + (1 - core)) & (c == mark))
+        def _():
+            pl.semaphore_signal(turn, inc=1, device_id={"expert": mate}, device_id_type=MESH)
+
         @pl.when((to == s) & (c == 0))
         def _():
             pltpu.make_async_copy(
@@ -325,15 +336,33 @@
         change = inv[None] * weighted - h * (inv * inv * inv * dot)[None]
         return (g.astype(F32) + change).astype(BF16)
 
-    columns(own, info_ref)
-    stage_full = [False]
+
+    def later_tables():
+        columns(own, info_ref)
+        for m in range(micro):
+            build(own, m)
+
+        @pl.when(s < last)
+        def _():
+            tell(1, s).wait_recv()
+            columns(after, info_near.at[1])
+            for m in range(micro):
+                build(after, m)
+
+            @pl.when(s == last - 1)
+            def _():
+                for m in range(micro):
+                    build_spread(m, info_near.at[1], micro)
 
     @pl.when(s > 0)
     def _():
+        build_spread(1)
+        pl.semaphore_wait(entered.at[0], 1)
         tell(0, s).wait_recv()
         columns(prev, info_near.at[0])
         for m in range(micro):
             build(prev, m)
+        later_tables()
 
     def forward(m, carry):
         u = m
@@ -352,7 +381,8 @@
         for q in range(PARTS):
             gain = info_ref[2 * micro + q : 2 * micro + q + 1, :]
             stage[pl.ds(q * tok, tok), :] = (h_in[m, q].astype(F32) * inv * gain).astype(BF16)
-        dispatch(u, m)
+        fill(u, spread[m, :, :n] + spread[m, :, n:], stage[:n, :])
+        dispatch(u)
 
         @pl.when(s < last)
         def _():
@@ -368,15 +398,14 @@
                 copy.wait()
             for copy in remote:
                 copy.wait_recv()
-            for i in range(micro):
-                build(own, i)
+
+            @pl.when(s == 0)
+            def _():
+                build_spread(1)
 
             @pl.when(s < last)
             def _():
-                tell(1, s).wait_recv()
-                columns(after, info_near.at[1])
-                for i in range(micro):
-                    build(after, i)
+                pl.semaphore_wait(entered.at[1], 1)
 
         def chunk(c, carry):
             arrive(u, c)
@@ -398,36 +427,53 @@
                 return carry
 
             lax.fori_loop(0, PARTS, second, 0)
-            give_back(u, c, jnp.minimum(s + 1, last), m + micro * (1 - behind))
+            give_back(u, c, jnp.where(s == last, last - 1, s + 1), m + micro * (1 - behind))
             return carry
 
         lax.fori_loop(0, CHUNKS, chunk, 0)
 
-        @pl.when(s == last)
-        def _():
-            g_in[m] = mix(h_in[m], micro + m, own, m)
-
         return carry
 
     lax.fori_loop(0, micro, forward, 0)
-    stage_full[0] = True
+
+    def scale(value, which, m):
+        upstream = value.astype(F32).reshape(n, part)
+        gates = gate_column(which, m)
+        stage[:n, :] = (gates[:n] * upstream).astype(BF16)
+        stage[n:, :] = (gates[n:] * upstream).astype(BF16)
+
+    @pl.when(s == last - 1)
+    def _():
+        def one(m, carry):
+            h_back(m=m, to=s).wait_recv()
+            g_next[m] = mix(h_next[m], micro + m, after, m)
+            scale(g_next[m], after, m)
+            fill(2 * micro + m, spread[micro + m], stage[...])
+            dispatch_last(m)
+            return carry
+
+        lax.fori_loop(0, micro, one, 0)
+
+    @pl.when(s == 0)
+    def _():
+        later_tables()
 
     def backward(m, carry):
         u = micro + m
 
-        @pl.when(s < last)
+        @pl.when(s < last - 1)
         def _():
             g_back(m=m, to=s).wait_recv()
             h_back(m=m, to=s).wait_recv()
+
+        @pl.when(s < last)
+        def _():
             g_in[m] = grad(g_next[m], h_next[m], info_near.at[1], 2 * micro + m, after, m)
-
-        upstream = g_in[m].astype(F32).reshape(n, part)
-        gates = gate_column(own, m)
-        stage[:n, :] = (gates[:n] * upstream).astype(BF16)
-        stage[n:, :] = (gates[n:] * upstream).astype(BF16)
-        dispatch(u, m)
-
-        @pl.when(s > 0)
+            scale(g_in[m], own, m)
+            fill(u, spread[m], stage[...])
+            dispatch(u)
+
+        @pl.when((s > 0) & (s < last))
         def _():
             g_back(m=m, to=s - 1).start()
 
@@ -492,8 +538,11 @@
         tell(1, s).wait_send()
 
     def drain(u, carry):
-        send_wait(send_a, u, a_send, chips - 1)
-        stays = jnp.where(u < micro, s == last, s == 0)
+        @pl.when(u < turns)
+        def _():
+            send_wait(send_a, u, a_send, chips - 1)
+
+        stays = (u >= micro) & (s == 0)
 
         @pl.when(stays)
         def _():
@@ -516,7 +565,14 @@
         @pl.when(s > 0)
         def _():
             h_back(m=m, to=s).wait_send()
+
+        @pl.when((s > 0) & (s < last))
+        def _():
             g_back(m=m, to=s).wait_send()
+
+        @pl.when(s == last - 1)
+        def _():
+            send_wait(send_a, 2 * micro + m, a_send, chips)
 
 
 def body(tokens, norm_gain, w_gate, w_up, w_down, route_ids, route_gates):
@@ -576,10 +632,12 @@
             pltpu.VMEM((3, top * PARTS * tok, 16), F32),
         ]
         + [pltpu.VMEM((micro, PARTS, tok, part), BF16)] * 6
-        + [pltpu.VMEM((units, chips, blk, part), BF16)] * 3
         + [
+            pltpu.VMEM((units + micro, chips, blk, part), BF16),
+            pltpu.VMEM((units, chips, blk, part), BF16),
+            pltpu.VMEM((units, chips, blk, part), BF16),
             pltpu.VMEM((2 * units, chips, blk, part), BF16),
-            pltpu.VMEM((micro, chips * blk, top * PARTS * tok), BF16),
+            pltpu.VMEM((2 * micro, chips * blk, top * PARTS * tok), BF16),
             pltpu.VMEM((3, micro, top * PARTS * tok, chips * blk), BF16),
             pltpu.VMEM((top * PARTS * tok, part), BF16),
             pltpu.VMEM((groups // CHUNKS, PARTS * grp, part), BF16),
@@ -593,13 +651,14 @@
             dma((3,)),
             dma((2,)),
             dma((2,)),
-            dma((units,)),
+            dma((units + micro,)),
             dma((units, groups)),
             dma((units,)),
             dma((2 * units, groups)),
             dma((4, micro)),
             dma((4, micro)),
             pltpu.SemaphoreType.REGULAR,
+            pltpu.SemaphoreType.REGULAR((2,)),
         ],
         compiler_params=pltpu.CompilerParams(
             collective_id=0, has_side_effects=True, vmem_limit_bytes=60 * 1024 * 1024

time: 456 us -> 439 us (0.963)
  Pallas kernels: 449 us -> 432 us
    pallas_call x1, Pallas kernels: 449 us -> 432 us  [body(): pl.pallas_call(functools.partial(kernel, dims), out_shape=jax.ShapeDtypeS...]
where the time goes in v6:
time: 439 us
  Pallas kernels  432 us (98%)
    pallas_call x1, Pallas kernels, body(): pl.pallas_call(functools.partial(kernel, dims), out_shape=jax.ShapeDtypeS...  432 us

profile of v6, /device:TPU:1, one launch (start us, length us, event | category | flops | bytes accessed | tf_op | source)
XLA Modules:
  0.0 439.2 jit_solution(1391197744584817534)
XLA Ops:
  0.0 0.1 pad.12.clone
  0.1 0.1 add.105
  0.2 0.1 add.106
  0.3 0.7 broadcast_in_dim.6
  0.9 0.1 reshape.93
  1.0 0.7 reduce
  1.8 0.8 copy.8
  2.6 0.1 eq.44
  2.7 0.1 fusion.2
  2.8 0.2 reduce_window_sum.11
  3.0 0.2 select_reduce_fusion
  3.2 0.1 reduce_sum.12
  3.4 0.1 copy.10
  3.5 0.1 add.104
  3.6 0.7 fusion.5.info_ref
  4.2 0.7 fusion.1
  5.0 432.3 %relay.1 = bf16[2,64,2560]{2,1,0:T(8,128)(2,1)} custom-call(bf16[2,64,2560]{2,1,0:T(8,128)(2,1)} %tokens_ref.1, f32[16,640]{1,0:T(8,128)} %fusion.5.info_ref, bf16[192,192]{1,0:T(8,128)(2,1)} %get-tuple-element.6.perm_ref, bf16[192,192]{1,0:T(8,128)(2,1)} %get-tuple-element.5.perm_t_ref, bf16[2560,384]{1,0:T(8,128)(2,1)} %bitcast.16, ...), custom_call_target="tpu_custom_call" | custom-call | tf_op jit(solution)/shard_map/relay/pallas_call | solution.py:622
  437.3 2.0 copy.12
  (7 shorter events, 0.1 us)

commit v7 on v6

--- a/solution.py
+++ b/solution.py
@@ -2,6 +2,7 @@
 
 import jax
 import jax.numpy as jnp
+import numpy as np
 from jax import lax
 from jax.experimental import pallas as pl
 from jax.experimental.pallas import tpu as pltpu
@@ -80,7 +81,7 @@
     hidden = 2 * half
     n = PARTS * tok
     step = 256
-    mark = 1
+    mark = 2
     last = sections - 1
     prev, own, after = 0, 1, 2
     s = lax.axis_index("section")
@@ -610,10 +611,10 @@
         ]
     )
 
-    src = jnp.arange(per * blk, dtype=jnp.int32)
+    src = np.arange(per * blk)
     dest = (src % blk // cap) * grp + src // blk * cap + src % cap
-    perm_t = (dest[:, None] == src[None, :]).astype(BF16)
-    perm = (src[:, None] == dest[None, :]).astype(BF16)
+    perm_t = jnp.asarray(dest[:, None] == src[None, :], dtype=BF16)
+    perm = jnp.asarray(src[:, None] == dest[None, :], dtype=BF16)
 
     dims = (sections, chips, cap, tok, width, micro, groups, half)
     vmem = pl.BlockSpec(memory_space=pltpu.VMEM)

time: 439 us -> 439 us (level)
  no operation moved by 1% of the time
where the time goes in v7:
time: 439 us
  Pallas kernels  433 us (99%)
    pallas_call x1, Pallas kernels, body(): pl.pallas_call(functools.partial(kernel, dims), out_shape=jax.ShapeDtypeS...  433 us

profile of v7, /device:TPU:1, one launch (start us, length us, event | category | flops | bytes accessed | tf_op | source)
XLA Modules:
  0.0 438.8 jit_solution(17294056987779737712)
XLA Ops:
  0.0 0.1 pad.12.clone
  0.1 0.1 add.31
  0.2 0.1 add.32
  0.2 0.7 broadcast_in_dim.6
  0.9 0.1 reshape.21
  1.0 0.7 reduce
  1.8 0.8 copy.10
  2.5 0.1 eq.15
  2.7 0.1 fusion
  2.8 0.2 reduce_window_sum.11
  3.0 0.2 select_reduce_fusion
  3.2 0.1 reduce_sum.12
  3.3 0.1 copy.12
  3.4 0.1 add.30
  3.5 0.7 fusion.3.info_ref
  4.2 432.6 %relay.1 = bf16[2,64,2560]{2,1,0:T(8,128)(2,1)} custom-call(bf16[2,64,2560]{2,1,0:T(8,128)(2,1)} %tokens_ref.1, f32[16,640]{1,0:T(8,128)} %fusion.3.info_ref, bf16[192,192]{1,0:T(8,128)(2,1)} %constant.18.clone.perm_ref, bf16[192,192]{1,0:T(8,128)(2,1)} %constant.17.clone.perm_t_ref, bf16[2560,384]{1,0:T(8,128)(2,1)} %bitcast.16, ...), custom_call_target="tpu_custom_call" | custom-call | tf_op jit(solution)/shard_map/relay/pallas_call | solution.py:623
  436.8 2.0 copy.14
  (6 shorter events, 0.0 us)
